TPU v7x, 128 devices: a whole 4x4x4 slice. The times are simulated.
128 devices in a mesh: lon: 32 (over z, y, core), lat: 4 (over x).
Axes of the slice: x: 4, y: 4, z: 4, core: 2. Of those that a mesh axis runs over, the one named last changes fastest.
Arguments:
- forcing: float32 [75, 256, 4096], P(None, 'lat', 'lon'), may hold values from -6 to 6
- obs_values: float32 [75, 1048576], P(None, ('lon', 'lat')), may hold values from -6 to 6
- obs_owner: int32 [1048576], P(('lon', 'lat')), may hold values from 0 to 127, as said below
- obs_cell: int32 [1048576], P(('lon', 'lat')), may hold values from 0 to 8191
- obs_count: int32 [128], P(('lon', 'lat')), may hold values from 1024 to 8192, as said below
- coef_east: float32 [256, 4096], P('lat', 'lon'), may hold values from 0.05 to 0.11
- coef_north: float32 [256, 4096], P('lat', 'lon'), may hold values from 0.05 to 0.11
- area_inv: float32 [256, 4096], P('lat', 'lon'), may hold values from 0.6 to 2
- sea_mask: int32 [256, 4096], P('lat', 'lon'), may hold values 0 or 1
- vert_coef: float32 [74], replicated, may hold values from 0.3 to 0.5
- inv_thick: float32 [75], replicated, may hold values from 0.5 to 0.7
Outputs:
- adjoint_field: float32 [75, 256, 4096], P(None, 'lat', 'lon')
Inputs may be any that keep to these rules, and one draw needn't show every extreme that they name: `obs_owner`: owners are numbered lon index times the number of lat devices plus lat index. Among the slots of one device at most 64 go to one owner, and in every draw some owner receives 64 used slots from every device. `obs_count`: slots of a device at or past its count are unused and ignored.
All inputs are finite; a program needn't handle non-finite values. No bound on the sum of `sea_mask` on one device may be relied on, other than what follows from the above.
Results may differ from a plain program's by a relative error of at most 0.0003.
Values sent between devices are 32-bit elements; how exact they have to be, the bound alone decides.
A program may use at most 128 MiB of HBM per device.

v0:
```python
import jax
import jax.numpy as jnp
from jax import lax
from jax.sharding import PartitionSpec as P

STEPS = 4


def padded_2(x, sides, width, wrap):
    for axis, dim in sides:
        size, length = (lax.axis_size(axis), x.shape[dim])
        up = [(i, (i + 1) % size) for i in range(size if wrap else size - 1)]
        down = [(j, i) for i, j in up]
        last = lax.slice_in_dim(x, length - width, length, axis=dim)
        initial = lax.slice_in_dim(x, 0, width, axis=dim)
        before = lax.ppermute(last, axis, up)
        after = lax.ppermute(initial, axis, down)
        x = jnp.concatenate([before, x, after], axis=dim)
    return x


def vertical_inverse(vert_coef, inv_thick):
    empty = jnp.zeros((1,), jnp.float32)
    upper_c = jnp.concatenate([vert_coef, empty])
    lower_c = jnp.concatenate([empty, vert_coef])
    middle = 1.0 + (lower_c + upper_c) * inv_thick
    above = jnp.concatenate([-inv_thick[1:] * vert_coef, empty])
    below = jnp.concatenate([empty, -inv_thick[:-1] * vert_coef])
    ident = jnp.eye(inv_thick.shape[0], dtype=jnp.float32)
    return lax.linalg.tridiagonal_solve(below, middle, above, ident)


def edge_parts(padded):
    east_coef = padded[0]
    north_coef = padded[1]
    sea_pad = padded[3]
    middle = sea_pad[1:-1, 1:-1]
    east_edge = east_coef[1:-1, 1:-1] * middle * sea_pad[1:-1, 2:]
    west_edge = east_coef[1:-1, :-2] * sea_pad[1:-1, :-2] * middle
    north_edge = north_coef[1:-1, 1:-1] * middle * sea_pad[2:, 1:-1]
    south_edge = north_coef[:-2, 1:-1] * sea_pad[:-2, 1:-1] * middle
    return (east_edge, west_edge, north_edge, south_edge)


def column_solve(matrix, values):
    extent = values.shape
    product = jnp.dot(
        matrix,
        values.reshape(extent[0], -1),
        precision=lax.Precision.HIGHEST,
        preferred_element_type=jnp.float32,
    )
    return product.reshape(extent)


def spread(values, area, edges):
    east_edge, west_edge, north_edge, south_edge = edges
    weighted = area * values
    centre = weighted[:, 1:-1, 1:-1]
    return (
        values[:, 1:-1, 1:-1]
        + east_edge * (weighted[:, 1:-1, 2:] - centre)
        + west_edge * (weighted[:, 1:-1, :-2] - centre)
        + north_edge * (weighted[:, 2:, 1:-1] - centre)
        + south_edge * (weighted[:, :-2, 1:-1] - centre)
    )


def local(
    forcing,
    obs_values,
    obs_owner,
    obs_cell,
    obs_count,
    coef_east,
    coef_north,
    area_inv,
    sea_mask,
    vert_coef,
    inv_thick,
):
    levels, rows_dev, cols_dev = forcing.shape
    lon_count = lax.axis_size("lon")
    lat_count = lax.axis_size("lat")
    devices = lon_count * lat_count
    obs_rows = obs_owner.shape[0]
    capacity = obs_rows // devices
    active = jnp.arange(obs_rows, dtype=jnp.int32) < obs_count[0]
    targets = jnp.arange(devices, dtype=jnp.int32)
    onehot = ((obs_owner[:, None] == targets[None, :]) & active[:, None]).astype(jnp.bfloat16)
    block_rows = min(512, obs_rows)
    block_count = obs_rows // block_rows
    grouped = onehot.reshape(block_count, block_rows, devices)
    lower_ones = (jnp.arange(block_rows)[:, None] >= jnp.arange(block_rows)[None, :]).astype(
        jnp.bfloat16
    )
    within = jnp.einsum("rs,bsd->brd", lower_ones, grouped, preferred_element_type=jnp.float32)
    totals = within[:, -1, :]
    offsets = jnp.cumsum(totals, axis=0) - totals
    rank_all = within + offsets[:, None, :] - 1.0
    slot_index = (
        jnp.sum(jnp.where(grouped > 0, rank_all, 0.0), axis=-1).reshape(obs_rows).astype(jnp.int32)
    )
    send_place = jnp.where(active, obs_owner * capacity + slot_index, obs_rows)
    send_values = (
        jnp.zeros((levels, obs_rows), jnp.float32).at[:, send_place].set(obs_values, mode="drop")
    )
    send_cells = jnp.zeros((1, obs_rows), jnp.int32).at[0, send_place].set(obs_cell, mode="drop")
    got_values, got_cells = (
        lax.all_to_all(send_values, ("lon", "lat"), split_axis=1, concat_axis=1, tiled=True),
        lax.all_to_all(send_cells, ("lon", "lat"), split_axis=1, concat_axis=1, tiled=True),
    )
    adjoint = (
        forcing.reshape(levels, rows_dev * cols_dev)
        .at[:, got_cells[0]]
        .add(got_values)
        .reshape(forcing.shape)
    )
    matrix = vertical_inverse(vert_coef, inv_thick)
    stacked = jnp.stack([coef_east, coef_north, area_inv, sea_mask.astype(jnp.float32)])
    depth = 1
    coef_wide = padded_2(stacked, (("lon", 2),), depth, True)
    padded = padded_2(coef_wide, (("lat", 1),), depth, False)
    outer_edges = edge_parts(padded)
    area_pad = padded[2]

    def single(index, state):
        state = column_solve(matrix, state)
        widened = padded_2(state, (("lon", 2),), 1, True)
        extended = padded_2(widened, (("lat", 1),), 1, False)
        return spread(extended, area_pad, outer_edges)

    adjoint = lax.fori_loop(0, STEPS, single, adjoint)
    return adjoint


def solution(mesh):
    in_specs = (
        P(None, "lat", "lon"),
        P(None, ("lon", "lat")),
        P(("lon", "lat")),
        P(("lon", "lat")),
        P(("lon", "lat")),
        P("lat", "lon"),
        P("lat", "lon"),
        P("lat", "lon"),
        P("lat", "lon"),
        P(),
        P(),
    )
    out_specs = P(None, "lat", "lon")
    return jax.shard_map(local, mesh=mesh, in_specs=in_specs, out_specs=out_specs, check_vma=False)
```

profile of v0, /device:TPU:0, one launch (start us, length us, event | category | flops | bytes accessed | tf_op | source)
XLA Modules:
  0.0 631.0 jit_solution(9418530992535122818)
XLA Ops:
  1.7 6.1 collective-permute-start.5
  15.5 4.2 select_reduce_fusion
  20.1 30.7 %scatter_custom_fusion.2 = s32[8192]{0:T(1024)S(1)} fusion(s32[8192]{0:T(1024)S(1)} %broadcast_select_fusion, s32[8192]{0:T(1024)} %param.20, s32[]{:T(128)} %copy.93), kind=kCustom, calls=%fused_computation.290 | custom fusion | bytes 33280
  51.5 7.0 %all-to-all-start = ((s32[1,128,64]{2,0,1:T(1,128)}), s32[1,128,64]{2,0,1:T(1,128)S(1)}, u32[]{:S(2)}, u32[]{:S(2)}) async-start(s32[1,128,64]{2,0,1:T(1,128)} %bitcast.299), calls=%async_computation | async-start | bytes 131072 | tf_op jit(solution)/shard_map/all_to_all | solution.py:111
  63.2 169.3 %while.42 = (s32[]{:T(128)}, f32[]{:T(128)}, f32[75]{0:T(128)S(1)}, f32[2,32]{1,0:T(2,128)S(1)}, f32[2,32,75]{2,1,0:T(8,128)S(1)}, /*index=5*/f32[2,32]{1,0:T(2,...) while((s32[]{:T(128)}, f32[]{:T(128)}, f32[75]{0:T(128)S(1)}, ...), condition=%wide.region_6.7_spmd, body=%wide.region_5.6_spmd.sunk | while | flops 7329 | bytes 76413 | solution.py:30
  127.5 20.1 %fusion.341 = (f32[75]{0:T(128)S(1)}, f32[75]{0:T(128)S(1)}, f32[75]{0:T(128)S(1)}, f32[75]{0:T(128)S(1)}, f32[75]{0:T(128)S(1)}, /*index=5*/f32[75]{0:T(128)S(1...) fusion(f32[2,32,75]{2,1,0:T(8,128)S(1)} %get-tuple-element.1173, ...), kind=kLoop, calls=%fused_computation.44.clone.1 | loop fusion | flops 7200 | bytes 19884 | tf_op jit(solution)/shard_map/while/body/eval_jaxpr/div | solution.py:30
  212.1 20.1 %fusion.341 = (f32[75]{0:T(128)S(1)}, f32[75]{0:T(128)S(1)}, f32[75]{0:T(128)S(1)}, f32[75]{0:T(128)S(1)}, f32[75]{0:T(128)S(1)}, /*index=5*/f32[75]{0:T(128)S(1...) fusion(f32[2,32,75]{2,1,0:T(8,128)S(1)} %get-tuple-element.1173, ...), kind=kLoop, calls=%fused_computation.44.clone.1 | loop fusion | flops 7200 | bytes 19884 | tf_op jit(solution)/shard_map/while/body/eval_jaxpr/div | solution.py:30
  251.5 6.2 fusion.209
  257.8 43.5 %while.43 = (s32[]{:T(128)}, f32[75]{0:T(128)S(1)}, f32[2,32,75]{2,1,0:T(8,128)S(1)}, f32[2,32,75]{2,1,0:T(8,128)S(1)}, f32[2,32]{1,0:T(2,128)S(1)}, /*index=5*/...) while((s32[]{:T(128)}, f32[75]{0:T(128)S(1)}, ...), condition=%wide.region_8.9_spmd, body=%wide.region_7.8_spmd.sunk | while | flops 4834 | bytes 73553 | solution.py:30
  259.3 20.2 %fusion.344 = (f32[75]{0:T(128)S(1)}, f32[75]{0:T(128)S(1)}, f32[75]{0:T(128)S(1)}, f32[75]{0:T(128)S(1)}, f32[75]{0:T(128)S(1)}, /*index=5*/f32[75]{0:T(128)S(1...) fusion(f32[2,32,75]{2,1,0:T(8,128)S(1)} %get-tuple-element.1286, ...), kind=kLoop, calls=%fused_computation.172.clone.1 | loop fusion | flops 4800 | bytes 19756 | tf_op jit(solution)/shard_map/while/body/eval_jaxpr/sub | solution.py:30
  281.0 20.2 %fusion.344 = (f32[75]{0:T(128)S(1)}, f32[75]{0:T(128)S(1)}, f32[75]{0:T(128)S(1)}, f32[75]{0:T(128)S(1)}, f32[75]{0:T(128)S(1)}, /*index=5*/f32[75]{0:T(128)S(1...) fusion(f32[2,32,75]{2,1,0:T(8,128)S(1)} %get-tuple-element.1286, ...), kind=kLoop, calls=%fused_computation.172.clone.1 | loop fusion | flops 4800 | bytes 19756 | tf_op jit(solution)/shard_map/while/body/eval_jaxpr/sub | solution.py:30
  308.6 3.4 copy.36
  312.0 23.1 %scatter_custom_fusion = f32[75,8192]{0,1:T(8,128)} fusion(s32[8192]{0:T(1024)S(1)} %compare_select_fusion.1, f32[8192,75]{1,0:T(8,128)} %copy.36, f32[]{:T(128)} %constant.78.clone.1), kind=kCustom, calls=%fused_computation.259 | custom fusion | bytes 2458112 | tf_op jit(solution)/shard_map/scatter | solution.py:106
  335.2 2.7 collective-permute-start.6
  339.2 12.0 %all-to-all-start.1 = ((f32[75,128,64]{0,2,1:T(8,128)}), f32[75,128,64]{0,2,1:T(8,128)}, u32[]{:S(2)}, u32[]{:S(2)}) async-start(f32[75,128,64]{0,2,1:T(8,128)} %bitcast.1353), calls=%async_computation.1 | async-start | bytes 8388608 | tf_op jit(solution)/shard_map/all_to_all | solution.py:110
  352.5 3.5 copy.32
  358.1 45.7 %all-to-all-done.1 = f32[75,128,64]{0,2,1:T(8,128)} async-done(((f32[75,128,64]{0,2,1:T(8,128)}), f32[75,128,64]{0,2,1:T(8,128)}, u32[]{:S(2)}, u32[]{:S(2)}) %all-to-all-start.1) | async-done | bytes 2457632 | tf_op jit(solution)/shard_map/all_to_all | solution.py:110
  403.8 52.2 %scatter_fusion = f32[75,8192]{0,1:T(8,128)} fusion(f32[75,8192]{0,1:T(8,128)} %bitcast.1351, s32[8192]{0:T(1024)S(1)} %bitcast.1375, f32[8192,75]{1,0:T(8,128)} %bitcast.304), kind=kCustom, calls=%fused_computation.1 | custom fusion | flops 614400 | bytes 7405568 | tf_op jit(solution)/shard_map/scatter-add | solution.py:116
  456.1 5.2 copy.37
  461.2 165.8 %while.44 = (s32[]{:T(128)}, f32[75,64,128]{2,0,1:T(8,128)}, f32[75,75]{1,0:T(8,128)S(1)}, f32[64,128]{1,0:T(8,128)S(1)}, f32[1,66,130]{2,1,0:T(8,128)S(1)}, /*i...) while((s32[]{:T(128)}, f32[75,64,128]{2,0,1:T(8,128)}, ...), condition=%wide.region_10.11_spmd, body=%wide.region_9.10_spmd.sunk | while | flops 563589248 | bytes 40554944 | solution.py:133
  464.1 3.6 fusion.347
  467.7 3.2 fusion.348
  473.5 2.6 copy.54
  479.1 3.8 collective-permute-done.1
  487.5 4.6 collective-permute-start.3
  494.1 4.3 maximum_multiply_fusion.2
  498.5 3.9 fusion.349
  505.2 3.6 fusion.347
  508.9 3.2 fusion.348
  514.7 2.6 copy.54
  520.2 3.8 collective-permute-done.1
  528.7 4.9 collective-permute-start.3
  535.7 4.3 maximum_multiply_fusion.2
  540.0 3.9 fusion.349
  546.8 3.6 fusion.347
  550.4 3.2 fusion.348
  556.2 2.6 copy.54
  561.8 3.8 collective-permute-done.1
  570.2 4.9 collective-permute-start.3
  577.2 4.3 maximum_multiply_fusion.2
  581.6 3.9 fusion.349
  588.3 3.6 fusion.347
  592.0 3.2 fusion.348
  603.3 3.8 collective-permute-done.1
  611.8 4.9 collective-permute-start.3
  618.8 4.3 maximum_multiply_fusion.2
  623.1 3.9 fusion.349
  627.0 4.0 copy.38
  (171 shorter events, 101.5 us)
Async XLA Ops:
  1.7 333.4 %collective-permute-start.4 = (f32[4,64,1]{2,1,0:T(8,128)S(1)}, f32[4,64,1]{2,1,0:T(8,128)S(1)}, u32[]{:S(2)}, u32[]{:S(2)}) collective-permute-start(f32[4,64,1]{2,1,0:T(8,128)S(1)} %get-tuple-element.502), channel_id=1, source_target_pairs={{0,4},{4,8},{8,12},{12,16},{16,20},{20,24},{24,28},{28,32},{32,36}... | collective-permute-start | bytes 3080 | tf_op jit(solution)/shard_map/ppermute | solution.py:16
  1.7 333.3 %collective-permute-start.5 = (f32[4,64,1]{2,1,0:T(8,128)S(1)}, f32[4,64,1]{2,1,0:T(8,128)S(1)}, u32[]{:S(2)}, u32[]{:S(2)}) collective-permute-start(f32[4,64,1]{2,1,0:T(8,128)S(1)} %get-tuple-element.503), channel_id=1, source_target_pairs={{4,0},{8,4},{12,8},{16,12},{20,16},{24,20},{28,24},{32,28},{36,32}... | collective-permute-start | bytes 3080 | tf_op jit(solution)/shard_map/ppermute | solution.py:17
  10.6 1.9 copy-start
  15.5 4.3 copy-start.6
  15.5 4.3 copy-start.10
  15.5 4.5 copy-start.9
  15.5 43.0 %copy-start.7 = (f32[75]{0:T(128)S(1)}, f32[75]{0:T(128)}, u32[]{:S(2)}) copy-start(f32[75]{0:T(128)} %param.27) | copy-start | bytes 904
  15.5 43.0 %copy-start.8 = (f32[74]{0:T(128)S(1)}, f32[74]{0:T(128)}, u32[]{:S(2)}) copy-start(f32[74]{0:T(128)} %param.26) | copy-start | bytes 892
  51.5 287.7 %all-to-all-start = ((s32[1,128,64]{2,0,1:T(1,128)}), s32[1,128,64]{2,0,1:T(1,128)S(1)}, u32[]{:S(2)}, u32[]{:S(2)}) async-start(s32[1,128,64]{2,0,1:T(1,128)} %bitcast.299), calls=%async_computation | async-start | bytes 131072 | tf_op jit(solution)/shard_map/all_to_all | solution.py:111
  63.2 245.4 %copy-start.1 = (f32[75,8192]{1,0:T(8,128)S(1)}, f32[75,8192]{1,0:T(8,128)}, u32[]{:S(2)}) copy-start(f32[75,8192]{1,0:T(8,128)} %param.18) | copy-start | bytes 7372804
  312.0 23.1 %copy-start.3 = (f32[64,128]{1,0:T(8,128)S(1)}, f32[64,128]{1,0:T(8,128)}, u32[]{:S(2)}) copy-start(f32[64,128]{1,0:T(8,128)} %param.24) | copy-start | bytes 98308
  312.0 23.1 %copy-start.4 = (f32[64,128]{1,0:T(8,128)S(1)}, f32[64,128]{1,0:T(8,128)}, u32[]{:S(2)}) copy-start(f32[64,128]{1,0:T(8,128)} %param.23) | copy-start | bytes 98308
  312.0 23.1 %copy-start.5 = (f32[64,128]{1,0:T(8,128)S(1)}, f32[64,128]{1,0:T(8,128)}, u32[]{:S(2)}) copy-start(f32[64,128]{1,0:T(8,128)} %param.22) | copy-start | bytes 98308
  335.2 21.1 %collective-permute-start.6 = (f32[4,1,130]{2,1,0:T(1,128)S(1)}, f32[4,1,130]{2,1,0:T(1,128)S(1)}, u32[]{:S(2)}, u32[]{:S(2)}) collective-permute-start(f32[4,1,130]{2,1,0:T(1,128)S(1)} %get-tuple-element.492), channel_id=1, source_target_pairs={{0,1},{1,2},{2,3},{4,5},{5,6},{6,7},{8,9},{9,10},{10,11},{12,13},{... | collective-permute-start | bytes 6248 | tf_op jit(solution)/shard_map/ppermute | solution.py:16
  337.9 18.4 %collective-permute-start.7 = (f32[4,1,130]{2,1,0:T(1,128)S(1)}, f32[4,1,130]{2,1,0:T(1,128)S(1)}, u32[]{:S(2)}, u32[]{:S(2)}) collective-permute-start(f32[4,1,130]{2,1,0:T(1,128)S(1)} %get-tuple-element.493), channel_id=1, source_target_pairs={{1,0},{2,1},{3,2},{5,4},{6,5},{7,6},{9,8},{10,9},{11,10},{13,12},{... | collective-permute-start | bytes 6248 | tf_op jit(solution)/shard_map/ppermute | solution.py:17
  339.2 13.3 %copy-start.2 = (f32[75,64,128]{2,1,0:T(8,128)S(1)}, f32[75,64,128]{2,1,0:T(8,128)}, u32[]{:S(2)}) copy-start(f32[75,64,128]{2,1,0:T(8,128)} %param.17) | copy-start | bytes 7372804
  339.2 64.6 %all-to-all-start.1 = ((f32[75,128,64]{0,2,1:T(8,128)}), f32[75,128,64]{0,2,1:T(8,128)}, u32[]{:S(2)}, u32[]{:S(2)}) async-start(f32[75,128,64]{0,2,1:T(8,128)} %bitcast.1353), calls=%async_computation.1 | async-start | bytes 8388608 | tf_op jit(solution)/shard_map/all_to_all | solution.py:110
  473.4 3.2 collective-permute-start
  476.1 6.7 %collective-permute-start.1 = (f32[75,64,1]{0,1,2:T(8,128)S(1)}, f32[75,64,1]{0,1,2:T(8,128)S(1)}, u32[]{:S(2)}, u32[]{:S(2)}) collective-permute-start(f32[75,64,1]{0,1,2:T(8,128)S(1)} %copy.54), channel_id=1, source_target_pairs={{0,4},{4,8},{8,12},{12,16},{16,20},{20,24},{24,28},{28,32},{32,36}... | collective-permute-start | bytes 57608 | tf_op jit(solution)/shard_map/while/body/eval_jaxpr/ppermute | solution.py:16
  486.2 6.3 %collective-permute-start.2 = (f32[75,1,130]{2,0,1:T(8,128)S(1)}, f32[75,1,130]{2,0,1:T(8,128)S(1)}, u32[]{:S(2)}, u32[]{:S(2)}) collective-permute-start(f32[75,1,130]{2,0,1:T(8,128)S(1)} %get-tuple-element.1079), channel_id=1, source_target_pairs={{1,0},{2,1},{3,2},{5,4},{6,5},{7,6},{9,8},{10,9},{11,10},{13,12},{... | collective-permute-start | bytes 117008 | tf_op jit(solution)/shard_map/while/body/eval_jaxpr/ppermute | solution.py:17
  487.5 6.6 %collective-permute-start.3 = (f32[75,1,130]{2,0,1:T(8,128)S(1)}, f32[75,1,130]{2,0,1:T(8,128)S(1)}, u32[]{:S(2)}, u32[]{:S(2)}) collective-permute-start(f32[75,1,130]{2,0,1:T(8,128)S(1)} %get-tuple-element.1080), channel_id=1, source_target_pairs={{0,1},{1,2},{2,3},{4,5},{5,6},{6,7},{8,9},{9,10},{10,11},{12,13},{... | collective-permute-start | bytes 117008 | tf_op jit(solution)/shard_map/while/body/eval_jaxpr/ppermute | solution.py:16
  514.6 3.2 collective-permute-start
  517.3 6.7 %collective-permute-start.1 = (f32[75,64,1]{0,1,2:T(8,128)S(1)}, f32[75,64,1]{0,1,2:T(8,128)S(1)}, u32[]{:S(2)}, u32[]{:S(2)}) collective-permute-start(f32[75,64,1]{0,1,2:T(8,128)S(1)} %copy.54), channel_id=1, source_target_pairs={{0,4},{4,8},{8,12},{12,16},{16,20},{20,24},{24,28},{28,32},{32,36}... | collective-permute-start | bytes 57608 | tf_op jit(solution)/shard_map/while/body/eval_jaxpr/ppermute | solution.py:16
  527.4 6.7 %collective-permute-start.2 = (f32[75,1,130]{2,0,1:T(8,128)S(1)}, f32[75,1,130]{2,0,1:T(8,128)S(1)}, u32[]{:S(2)}, u32[]{:S(2)}) collective-permute-start(f32[75,1,130]{2,0,1:T(8,128)S(1)} %get-tuple-element.1079), channel_id=1, source_target_pairs={{1,0},{2,1},{3,2},{5,4},{6,5},{7,6},{9,8},{10,9},{11,10},{13,12},{... | collective-permute-start | bytes 117008 | tf_op jit(solution)/shard_map/while/body/eval_jaxpr/ppermute | solution.py:17
  528.7 7.0 %collective-permute-start.3 = (f32[75,1,130]{2,0,1:T(8,128)S(1)}, f32[75,1,130]{2,0,1:T(8,128)S(1)}, u32[]{:S(2)}, u32[]{:S(2)}) collective-permute-start(f32[75,1,130]{2,0,1:T(8,128)S(1)} %get-tuple-element.1080), channel_id=1, source_target_pairs={{0,1},{1,2},{2,3},{4,5},{5,6},{6,7},{8,9},{9,10},{10,11},{12,13},{... | collective-permute-start | bytes 117008 | tf_op jit(solution)/shard_map/while/body/eval_jaxpr/ppermute | solution.py:16
  556.2 3.2 collective-permute-start
  558.8 6.7 %collective-permute-start.1 = (f32[75,64,1]{0,1,2:T(8,128)S(1)}, f32[75,64,1]{0,1,2:T(8,128)S(1)}, u32[]{:S(2)}, u32[]{:S(2)}) collective-permute-start(f32[75,64,1]{0,1,2:T(8,128)S(1)} %copy.54), channel_id=1, source_target_pairs={{0,4},{4,8},{8,12},{12,16},{16,20},{20,24},{24,28},{28,32},{32,36}... | collective-permute-start | bytes 57608 | tf_op jit(solution)/shard_map/while/body/eval_jaxpr/ppermute | solution.py:16
  568.9 6.7 %collective-permute-start.2 = (f32[75,1,130]{2,0,1:T(8,128)S(1)}, f32[75,1,130]{2,0,1:T(8,128)S(1)}, u32[]{:S(2)}, u32[]{:S(2)}) collective-permute-start(f32[75,1,130]{2,0,1:T(8,128)S(1)} %get-tuple-element.1079), channel_id=1, source_target_pairs={{1,0},{2,1},{3,2},{5,4},{6,5},{7,6},{9,8},{10,9},{11,10},{13,12},{... | collective-permute-start | bytes 117008 | tf_op jit(solution)/shard_map/while/body/eval_jaxpr/ppermute | solution.py:17
  570.2 7.0 %collective-permute-start.3 = (f32[75,1,130]{2,0,1:T(8,128)S(1)}, f32[75,1,130]{2,0,1:T(8,128)S(1)}, u32[]{:S(2)}, u32[]{:S(2)}) collective-permute-start(f32[75,1,130]{2,0,1:T(8,128)S(1)} %get-tuple-element.1080), channel_id=1, source_target_pairs={{0,1},{1,2},{2,3},{4,5},{5,6},{6,7},{8,9},{9,10},{10,11},{12,13},{... | collective-permute-start | bytes 117008 | tf_op jit(solution)/shard_map/while/body/eval_jaxpr/ppermute | solution.py:16
  597.7 3.2 collective-permute-start
  600.4 6.7 %collective-permute-start.1 = (f32[75,64,1]{0,1,2:T(8,128)S(1)}, f32[75,64,1]{0,1,2:T(8,128)S(1)}, u32[]{:S(2)}, u32[]{:S(2)}) collective-permute-start(f32[75,64,1]{0,1,2:T(8,128)S(1)} %copy.54), channel_id=1, source_target_pairs={{0,4},{4,8},{8,12},{12,16},{16,20},{20,24},{24,28},{28,32},{32,36}... | collective-permute-start | bytes 57608 | tf_op jit(solution)/shard_map/while/body/eval_jaxpr/ppermute | solution.py:16
  610.5 6.7 %collective-permute-start.2 = (f32[75,1,130]{2,0,1:T(8,128)S(1)}, f32[75,1,130]{2,0,1:T(8,128)S(1)}, u32[]{:S(2)}, u32[]{:S(2)}) collective-permute-start(f32[75,1,130]{2,0,1:T(8,128)S(1)} %get-tuple-element.1079), channel_id=1, source_target_pairs={{1,0},{2,1},{3,2},{5,4},{6,5},{7,6},{9,8},{10,9},{11,10},{13,12},{... | collective-permute-start | bytes 117008 | tf_op jit(solution)/shard_map/while/body/eval_jaxpr/ppermute | solution.py:17
  611.8 7.0 %collective-permute-start.3 = (f32[75,1,130]{2,0,1:T(8,128)S(1)}, f32[75,1,130]{2,0,1:T(8,128)S(1)}, u32[]{:S(2)}, u32[]{:S(2)}) collective-permute-start(f32[75,1,130]{2,0,1:T(8,128)S(1)} %get-tuple-element.1080), channel_id=1, source_target_pairs={{0,1},{1,2},{2,3},{4,5},{5,6},{6,7},{8,9},{9,10},{10,11},{12,13},{... | collective-permute-start | bytes 117008 | tf_op jit(solution)/shard_map/while/body/eval_jaxpr/ppermute | solution.py:16
where the time goes:
time: 638 us; the launch traced here: 631 us
  other arithmetic  195 us (31%)
  local copies, waits for them, and re-layouts  155 us (24%)
  loops' own time  120 us (19%)
  waiting for transfers between devices  68.9 us (11%)
  starting transfers between devices  56 us (9%)
  between operations  20.5 us (3%)
  matrix products  15.8 us (2%)
    another operation x2, loops' own time, vertical_inverse(): return lax.linalg.tridiagonal_solve(below, middle, above, ident)  120 us
    scatter-add x1, other arithmetic, local(): adjoint = forcing.reshape(levels, rows_dev * cols_dev).at[:, got_cells[0]...  52.2 us
    div x4, other arithmetic, vertical_inverse(): return lax.linalg.tridiagonal_solve(below, middle, above, ident)  47.1 us
    all_to_all x1, waiting for transfers between devices, local(): lax.all_to_all(send_values, ('lon', 'lat'), split_axis=1, concat_axis=1,...  45.7 us
    sub x2, other arithmetic, vertical_inverse(): return lax.linalg.tridiagonal_solve(below, middle, above, ident)  40.4 us
    unnamed x26, local copies, waits for them, and re-layouts  39.6 us
    ppermute x10, starting transfers between devices, padded_2(): before = lax.ppermute(last, axis, up)  24.2 us
    scatter x1, local copies, waits for them, and re-layouts, local(): jnp.zeros((levels, obs_rows), jnp.float32).at[:, send_place]  23.1 us
  transfers between devices with their start and end apart: 22, of which 13 were waited for; matrix products, arithmetic and copies ran while one was open for 32% of the time, Pallas kernels for 0%

commit v1 on v0

v1 whole, which is shorter than its diff:
```python
import jax
import jax.numpy as jnp
from jax import lax
from jax.experimental import pallas as pl
from jax.experimental.pallas import tpu as pltpu
from jax.sharding import PartitionSpec as P

LEV = 75
LP = 80
NX = 128
NY = 64
DEV = 128
CAP = 64
SLOTS = 8192
ROWS = 40
HALO = 4
STRIDE = 53
F32 = jnp.float32
BF16 = jnp.bfloat16
HI = lax.Precision.HIGHEST
MESH = pl.DeviceIdType.MESH


def iota(shape, dim, dtype=jnp.int32):
    return lax.broadcasted_iota(dtype, shape, dim)


def vertical_body(vert_ref, thick_ref, out_ref, cp_ref, dp_ref):
    lane = iota((1, NX), 1)
    dp_ref[...] = jnp.zeros_like(dp_ref)

    def forward(i, carry):
        cp, dp = carry
        up = jnp.where(i < LEV - 1, vert_ref[jnp.minimum(i, LEV - 2)], 0.0)
        low = jnp.where(i > 0, vert_ref[jnp.maximum(i - 1, 0)], 0.0)
        middle = 1.0 + (low + up) * thick_ref[i]
        above = -thick_ref[jnp.minimum(i + 1, LEV - 1)] * up
        below = -thick_ref[jnp.maximum(i - 1, 0)] * low
        inv = 1.0 / (middle - below * cp)
        cp = above * inv
        dp = (jnp.where(lane == i, 1.0, 0.0) - below * dp) * inv
        cp_ref[pl.ds(i, 1), :] = cp
        dp_ref[pl.ds(i, 1), :] = dp
        return cp, dp

    zero = jnp.zeros((1, NX), F32)
    lax.fori_loop(0, LEV, forward, (zero, zero))

    def backward(j, x):
        i = LEV - 1 - j
        x = dp_ref[pl.ds(i, 1), :] - cp_ref[pl.ds(i, 1), :] * x
        dp_ref[pl.ds(i, 1), :] = x
        return x

    lax.fori_loop(0, LEV, backward, zero)
    single = dp_ref[...]
    double = jnp.dot(single, single, precision=HI, preferred_element_type=F32)
    out_ref[...] = jnp.dot(double, double, precision=HI, preferred_element_type=F32)


def vertical_fourth(vert_coef, inv_thick):
    return pl.pallas_call(
        vertical_body,
        out_shape=jax.ShapeDtypeStruct((NX, NX), F32),
        in_specs=[pl.BlockSpec(memory_space=pltpu.SMEM)] * 2,
        out_specs=pl.BlockSpec(memory_space=pltpu.VMEM),
        scratch_shapes=[pltpu.VMEM((NX, NX), F32), pltpu.VMEM((NX, NX), F32)],
        name="vertical",
    )(vert_coef, inv_thick)


def places_body(count_ref, own_ref, idx_ref):
    width = 256
    count = count_ref[0]
    lane = iota((1, width), 1)
    owners = iota((DEV, width), 0)
    tri = (iota((width, width + NX), 0) <= iota((width, width + NX), 1)) | (
        iota((width, width + NX), 1) >= width
    )
    tri = tri.astype(F32).astype(BF16)
    kth = iota((CAP, width), 0).astype(F32)
    number = (iota((CAP, width), 1) + 1).astype(F32)
    acc_lane = iota((DEV, NX), 1)

    def step(b, carry):
        offset, acc = carry
        own = jnp.concatenate([own_ref[pl.ds(2 * b, 1), :], own_ref[pl.ds(2 * b + 1, 1), :]], 1)
        own = jnp.where(lane + b * width < count, own, -1)
        onehot = jnp.where(jnp.broadcast_to(own, (DEV, width)) == owners, 1.0, 0.0)
        ones = onehot.astype(BF16)
        prefix = jnp.dot(ones, tri, preferred_element_type=F32)
        rank = prefix[:, :width] + jnp.concatenate([offset, offset], 1)
        rank = jnp.sum(onehot * rank, axis=0, keepdims=True) - 1.0
        hit = jnp.where(jnp.broadcast_to(rank, (CAP, width)) == kth, 1.0, 0.0)
        both = jnp.concatenate([hit, hit * number], 0).astype(BF16)
        found = lax.dot_general(ones, both, (((1,), (1,)), ((), ())), preferred_element_type=F32)
        scale = jnp.where(acc_lane < CAP, (b * width).astype(F32), 1.0)
        return offset + prefix[:, width:], acc + found * scale

    zero = jnp.zeros((DEV, NX), F32)
    _, acc = lax.fori_loop(0, SLOTS // width, step, (zero, zero), unroll=4)
    total = (acc + pltpu.roll(acc, CAP, 1)).astype(jnp.int32)
    idx_ref[...] = jnp.where(total > 0, total - 1, SLOTS)


def places(owner, count):
    return pl.pallas_call(
        places_body,
        out_shape=jax.ShapeDtypeStruct((DEV, NX), jnp.int32),
        in_specs=[
            pl.BlockSpec(memory_space=pltpu.SMEM),
            pl.BlockSpec(memory_space=pltpu.VMEM),
        ],
        out_specs=pl.BlockSpec(memory_space=pltpu.VMEM),
        name="places",
    )(count, owner.reshape(SLOTS // NX, NX))


def send_body(
    idx_ref, obs_ref, cell_ref, coef_ref,
    recv_ref, row_halo_ref, col_halo_ref, corner_ref,
    table, rows, outbox, colbox, send_sem, recv_sem, side_send, side_recv,
):
    lon = lax.axis_index("lon")
    lat = lax.axis_index("lat")
    z, y, c = lon // 8, (lon // 2) % 4, lon % 2
    me = lon * 4 + lat

    def target(k):
        q = (k * STRIDE) % DEV
        dx, dc, dy, dz = q % 4, (q // 4) % 2, (q // 8) % 4, q // 32
        return (((z + dz) % 4) * 4 + (y + dy) % 4) * 2 + (c + dc) % 2, (lat + dx) % 4

    barrier = pltpu.get_barrier_semaphore()

    def greet(k, _):
        pl.semaphore_signal(barrier, inc=1, device_id=target(k), device_id_type=MESH)
        return 0

    lax.fori_loop(1, DEV, greet, 0)

    def turn(b, _):
        columns = pl.ds(pl.multiple_of(b * NX, NX), NX)
        block = jnp.concatenate(
            [
                obs_ref[:, columns],
                cell_ref[pl.ds(b, 1), :].astype(F32),
                jnp.zeros((NX - LEV - 1, NX), F32),
            ],
            0,
        )
        table[columns, :] = block.T
        return 0

    lax.fori_loop(0, SLOTS // NX, turn, 0)
    table[pl.ds(SLOTS, 8), :] = jnp.zeros((8, NX), F32)

    lane = iota((NY, NX), 1)
    cols = jnp.zeros((NY, NX), F32)
    for i in range(4):
        cols = jnp.where((lane >= 8 * i) & (lane < 8 * i + 4), pltpu.roll(coef_ref[i], 8 * i, 1), cols)
        cols = jnp.where(
            (lane >= 8 * i + 4) & (lane < 8 * i + 8),
            pltpu.roll(coef_ref[i], (8 * i + 4 - 124) % NX, 1),
            cols,
        )
    colbox[...] = cols
    pl.semaphore_wait(barrier, DEV - 1)

    east, west = (lon + 1) % 32, (lon + 31) % 32
    north, south = (lat + 1) % 4, (lat + 3) % 4
    side = []

    def beside(number, src, dst, where):
        copy = pltpu.make_async_remote_copy(
            src_ref=src, dst_ref=dst, send_sem=side_send.at[number], recv_sem=side_recv.at[number],
            device_id=where, device_id_type=MESH,
        )
        copy.start()
        side.append(copy)

    beside(0, coef_ref.at[:, pl.ds(NY - 8, 8), :], row_halo_ref.at[0], (lon, north))
    beside(1, coef_ref.at[:, pl.ds(0, 8), :], row_halo_ref.at[1], (lon, south))
    beside(2, colbox, col_halo_ref.at[0], (east, lat))
    beside(3, colbox, col_halo_ref.at[1], (west, lat))
    beside(4, colbox.at[pl.ds(NY - 8, 8), :], corner_ref.at[0], (east, north))
    beside(5, colbox.at[pl.ds(NY - 8, 8), :], corner_ref.at[1], (west, north))
    beside(6, colbox.at[pl.ds(0, 8), :], corner_ref.at[2], (east, south))
    beside(7, colbox.at[pl.ds(0, 8), :], corner_ref.at[3], (west, south))

    lane8 = iota((8, NX), 1)
    lane32 = iota((32, NX), 1)

    def gather(owner):
        for k in range(CAP):
            rows[pl.ds(k, 1), :] = table[pl.ds(idx_ref[owner, k], 1), :]

    def fold(box):
        box[pl.ds(0, 32), :] = jnp.where(
            lane32 < 64, rows[pl.ds(0, 32), :], pltpu.roll(rows[pl.ds(32, 32), :], 64, 1)
        )
        rest = jnp.zeros((8, NX), F32)
        for g in range(8):
            piece = rows[pl.ds(8 * g, 8), :]
            shift = (16 * g - 64) % NX
            piece = pltpu.roll(piece, shift, 1) if shift else piece
            rest = jnp.where(lane8 // 16 == g, piece, rest)
        box[pl.ds(32, 8), :] = rest

    def send(k, _):
        dlon, dlat = target(k)
        owner = dlon * 4 + dlat
        gather(owner)
        fold(outbox.at[owner])
        pltpu.make_async_remote_copy(
            src_ref=outbox.at[owner], dst_ref=recv_ref.at[me], send_sem=send_sem, recv_sem=recv_sem,
            device_id=(dlon, dlat), device_id_type=MESH,
        ).start()
        return 0

    lax.fori_loop(1, DEV, send, 0)
    gather(me)
    fold(recv_ref.at[me])
    for copy in side:
        copy.wait()
    others = pl.ds(0, DEV - 1)
    pltpu.make_async_copy(outbox.at[others], outbox.at[others], send_sem).wait()
    pltpu.make_async_copy(recv_ref.at[others], recv_ref.at[others], recv_sem).wait()


def send_profiles(idx, obs, cell, coefs):
    vm = pl.BlockSpec(memory_space=pltpu.VMEM)
    return pl.pallas_call(
        send_body,
        out_shape=(
            jax.ShapeDtypeStruct((DEV, ROWS, NX), F32),
            jax.ShapeDtypeStruct((2, 4, 8, NX), F32),
            jax.ShapeDtypeStruct((2, NY, NX), F32),
            jax.ShapeDtypeStruct((4, 8, NX), F32),
        ),
        in_specs=[pl.BlockSpec(memory_space=pltpu.SMEM), vm, vm, vm],
        out_specs=(vm, vm, vm, vm),
        scratch_shapes=[
            pltpu.VMEM((SLOTS + 8, NX), F32),
            pltpu.VMEM((CAP, NX), F32),
            pltpu.VMEM((DEV, ROWS, NX), F32),
            pltpu.VMEM((NY, NX), F32),
            pltpu.SemaphoreType.DMA(()),
            pltpu.SemaphoreType.DMA(()),
            pltpu.SemaphoreType.DMA((8,)),
            pltpu.SemaphoreType.DMA((8,)),
        ],
        compiler_params=pltpu.CompilerParams(
            collective_id=0, has_side_effects=True, vmem_limit_bytes=48 << 20
        ),
        name="send_profiles",
    )(idx, obs, cell.reshape(SLOTS // NX, NX), coefs)


WAYS = 4


def add_body(recv_ref, forcing_ref, out_ref, full, acc0, acc1, acc2, acc3, cell_v, cell_s, sem):
    accs = (acc0, acc1, acc2, acc3)
    pick = jnp.where(
        iota((8, NX), 1) == 16 * iota((8, NX), 0) + (LEV - 64), 1.0, 0.0
    ).astype(F32)

    def cells(b, _):
        part = recv_ref[pl.ds(16 * b, 16), pl.ds(32, 8), :].reshape(NX, NX)
        found = lax.dot_general(
            pick, part, (((1,), (1,)), ((), ())), precision=HI, preferred_element_type=F32
        )
        cell_v[:, pl.ds(pl.multiple_of(b * NX, NX), NX)] = (found + 0.5).astype(jnp.int32)
        return 0

    lax.fori_loop(0, 8, cells, 0, unroll=True)
    copy = pltpu.make_async_copy(cell_v, cell_s, sem)
    copy.start()

    def unfold(s, _):
        rest = recv_ref[s, pl.ds(32, 8), :]
        lane8 = iota((8, NX), 1)
        for g in range(8):
            tail = pltpu.roll(rest, (64 - 16 * g) % NX, 1) if g != 4 else rest
            head = recv_ref[s, pl.ds(8 * (g % 4), 8), :]
            head = pltpu.roll(head, 64, 1) if g >= 4 else head
            full[pl.ds(s * CAP + 8 * g, 8), :] = jnp.where(lane8 < 64, head, tail)
        return 0

    lax.fori_loop(0, DEV, unfold, 0, unroll=2)

    def clear(i, _):
        at = pl.ds(pl.multiple_of(i * 64, 64), 64)
        for acc in accs:
            acc[at, :] = jnp.zeros((64, NX), F32)
        return 0

    lax.fori_loop(0, SLOTS // 64, clear, 0)
    copy.wait()
    per = DEV // WAYS

    def add(s, _):
        for g in range(8):
            for e in range(8):
                for w, acc in enumerate(accs):
                    src = s + w * per
                    cell = cell_s[g, src * 8 + e]
                    at = pl.ds(cell, 1)
                    acc[at, :] = acc[at, :] + full[pl.ds(src * CAP + 8 * g + e, 1), :]
        return 0

    lax.fori_loop(0, per, add, 0)

    def finish(y, _):
        at = pl.ds(pl.multiple_of(y * NX, NX), NX)
        total = (acc0[at, :] + acc1[at, :]) + (acc2[at, :] + acc3[at, :])
        total = total.T
        base = forcing_ref[pl.ds(y, LEV, stride=NY), :]
        out_ref[y, pl.ds(0, LEV), :] = total[:LEV] + base
        out_ref[y, pl.ds(LEV, LP - LEV), :] = jnp.zeros((LP - LEV, NX), F32)
        return 0

    lax.fori_loop(0, NY, finish, 0)


def add_profiles(recv, forcing):
    vm = pl.BlockSpec(memory_space=pltpu.VMEM)
    return pl.pallas_call(
        add_body,
        out_shape=jax.ShapeDtypeStruct((NY, LP, NX), F32),
        in_specs=[vm, vm],
        out_specs=vm,
        scratch_shapes=[pltpu.VMEM((SLOTS, NX), F32)] * 5
        + [
            pltpu.VMEM((8, 8 * DEV), jnp.int32),
            pltpu.SMEM((8, 8 * DEV), jnp.int32),
            pltpu.SemaphoreType.DMA(()),
        ],
        compiler_params=pltpu.CompilerParams(vmem_limit_bytes=56 << 20),
        name="add_profiles",
    )(recv, forcing.reshape(LEV * NY, NX))


YE = NY + 2 * HALO


def spread_body(
    field_ref, coef_ref, row_halo_ref, col_halo_ref, corner_ref,
    out_ref,
    main_a, main_b, side_a, side_b, east_box, west_box, from_west, from_east, corners,
    coef_main, coef_side, fac_main, fac_side, send_sem, recv_sem,
):
    lon = lax.axis_index("lon")
    lat = lax.axis_index("lat")
    east, west = (lon + 1) % 32, (lon + 31) % 32
    north, south = (lat + 1) % 4, (lat + 3) % 4
    peers = [
        (lon, north), (lon, south), (east, lat), (west, lat),
        (east, north), (west, north), (east, south), (west, south),
    ]
    barrier = pltpu.get_barrier_semaphore()
    for peer in peers:
        pl.semaphore_signal(barrier, inc=1, device_id=peer, device_id_type=MESH)

    lane80 = iota((LP, NX), 1)
    for h in range(2):

        def pack(j, carry, h=h):
            e, w = carry
            row = field_ref[32 * h + j]
            here = (lane80 // 4) == j
            e = jnp.where(here, pltpu.roll(row, 4 * j + 4, 1), e)
            w = jnp.where(here, pltpu.roll(row, 4 * j, 1), w)
            return e, w

        zero = jnp.zeros((LP, NX), F32)
        e, w = lax.fori_loop(0, 32, pack, (zero, zero))
        east_box[h] = e
        west_box[h] = w

    pl.semaphore_wait(barrier, 8)
    moves = [
        (field_ref.at[pl.ds(NY - HALO, HALO)], main_a.at[pl.ds(0, HALO)]),
        (field_ref.at[pl.ds(0, HALO)], main_a.at[pl.ds(NY + HALO, HALO)]),
        (east_box, from_west),
        (west_box, from_east),
        (east_box.at[1], corners.at[0]),
        (west_box.at[1], corners.at[1]),
        (east_box.at[0], corners.at[2]),
        (west_box.at[0], corners.at[3]),
    ]
    copies = []
    for number, (src, dst) in enumerate(moves):
        copy = pltpu.make_async_remote_copy(
            src_ref=src, dst_ref=dst, send_sem=send_sem.at[number], recv_sem=recv_sem.at[number],
            device_id=peers[number], device_id_type=MESH,
        )
        copy.start()
        copies.append(copy)

    lane72 = iota((NY, NX), 1)
    lane4 = iota((HALO, NX), 1)
    for i in range(4):
        coef_main[i, pl.ds(HALO, NY), :] = coef_ref[i]
        coef_main[i, pl.ds(0, HALO), :] = row_halo_ref[0, i, pl.ds(4, HALO), :]
        coef_main[i, pl.ds(NY + HALO, HALO), :] = row_halo_ref[1, i, pl.ds(0, HALO), :]

        def sides(lanes, left, right, i=i):
            return jnp.where(
                lanes < 64,
                pltpu.roll(right, (-8 * i) % NX, 1),
                pltpu.roll(left, (124 - 8 * i - 4) % NX, 1),
            )

        coef_side[i, pl.ds(HALO, NY), :] = sides(lane72, col_halo_ref[0], col_halo_ref[1])
        coef_side[i, pl.ds(0, HALO), :] = sides(lane4, corner_ref[0, pl.ds(4, HALO), :], corner_ref[1, pl.ds(4, HALO), :])
        coef_side[i, pl.ds(NY + HALO, HALO), :] = sides(lane4, corner_ref[2, pl.ds(0, HALO), :], corner_ref[3, pl.ds(0, HALO), :])
    outside = jnp.logical_or(
        (iota((YE, NX), 0) < HALO) & (lat == 0), (iota((YE, NX), 0) >= NY + HALO) & (lat == 3)
    )
    coef_main[3] = jnp.where(outside, 0.0, coef_main[3])
    coef_side[3] = jnp.where(outside, 0.0, coef_side[3])

    def shifts(main, side, lanes):
        first, last = lanes == 0, lanes == NX - 1
        main_e = pltpu.roll(jnp.where(first, side, main), NX - 1, 1)
        side_e = pltpu.roll(jnp.where(first, main, side), NX - 1, 1)
        main_w = pltpu.roll(jnp.where(last, side, main), 1, 1)
        side_w = pltpu.roll(jnp.where(last, main, side), 1, 1)
        return main_e, side_e, main_w, side_w

    lanes = iota((YE, NX), 1)
    sea_m, sea_s = coef_main[3], coef_side[3]
    area_m, area_s = coef_main[2], coef_side[2]
    sea_me, sea_se, _, _ = shifts(sea_m, sea_s, lanes)
    east_m = coef_main[0] * sea_m * sea_me
    east_s = coef_side[0] * sea_s * sea_se
    _, _, west_m, west_s = shifts(east_m, east_s, lanes)
    area_me, area_se, area_mw, area_sw = shifts(area_m, area_s, lanes)

    def upward(x):
        return pltpu.roll(x, YE - 1, 0)

    def downward(x):
        return pltpu.roll(x, 1, 0)

    for fac, coef, ee, ww, sea, area, area_e, area_w in (
        (fac_main, coef_main, east_m, west_m, sea_m, area_m, area_me, area_mw),
        (fac_side, coef_side, east_s, west_s, sea_s, area_s, area_se, area_sw),
    ):
        nn = coef[1] * sea * upward(sea)
        ss = downward(nn)
        fac[0] = 1.0 - area * (ee + ww + nn + ss)
        fac[1] = ee * area_e
        fac[2] = ww * area_w
        fac[3] = nn * upward(area)
        fac[4] = ss * downward(area)

    def own(y, _):
        main_a[y + HALO] = field_ref[y]
        return 0

    lax.fori_loop(0, NY, own, 0)
    for copy in copies:
        copy.wait()

    def unpack(j, _):
        for h in range(2):
            side_a[HALO + 32 * h + j] = jnp.where(
                lane80 < 64,
                pltpu.roll(from_east[h], (NX - 4 * j) % NX, 1),
                pltpu.roll(from_west[h], (124 - 4 * j + NX) % NX, 1),
            )
        return 0

    lax.fori_loop(0, 32, unpack, 0)
    for j in range(HALO):
        k = 28 + j
        side_a[j] = jnp.where(
            lane80 < 64,
            pltpu.roll(corners[1], (NX - 4 * k) % NX, 1),
            pltpu.roll(corners[0], (124 - 4 * k) % NX, 1),
        )
        side_a[NY + HALO + j] = jnp.where(
            lane80 < 64,
            pltpu.roll(corners[3], (NX - 4 * j) % NX, 1),
            pltpu.roll(corners[2], (124 - 4 * j) % NX, 1),
        )

    first80, last80 = lane80 == 0, lane80 == NX - 1
    for t in range(4):
        src_m, src_s = (main_a, side_a) if t % 2 == 0 else (main_b, side_b)
        dst_m, dst_s = (main_b, side_b) if t % 2 == 0 else (main_a, side_a)
        final = t == 3

        def row(y, _):
            main, side = src_m[y], src_s[y]

            def fac(ref, i):
                return jnp.broadcast_to(ref[i, pl.ds(y, 1), :], (LP, NX))

            main_e = pltpu.roll(jnp.where(first80, side, main), NX - 1, 1)
            main_w = pltpu.roll(jnp.where(last80, side, main), 1, 1)
            new = (
                fac(fac_main, 0) * main
                + fac(fac_main, 1) * main_e
                + fac(fac_main, 2) * main_w
                + fac(fac_main, 3) * src_m[y + 1]
                + fac(fac_main, 4) * src_m[y - 1]
            )
            if final:
                out_ref[y - HALO] = new
            else:
                dst_m[y] = new
                side_e = pltpu.roll(jnp.where(first80, main, side), NX - 1, 1)
                side_w = pltpu.roll(jnp.where(last80, main, side), 1, 1)
                dst_s[y] = (
                    fac(fac_side, 0) * side
                    + fac(fac_side, 1) * side_e
                    + fac(fac_side, 2) * side_w
                    + fac(fac_side, 3) * src_s[y + 1]
                    + fac(fac_side, 4) * src_s[y - 1]
                )
            return 0

        lax.fori_loop(1 + t, YE - 1 - t, row, 0)


def spread(field, coefs, row_halo, col_halo, corner):
    vm = pl.BlockSpec(memory_space=pltpu.VMEM)
    wide = pltpu.VMEM((YE, LP, NX), F32)
    box = pltpu.VMEM((2, LP, NX), F32)
    return pl.pallas_call(
        spread_body,
        out_shape=jax.ShapeDtypeStruct((NY, LP, NX), F32),
        in_specs=[vm] * 5,
        out_specs=vm,
        scratch_shapes=[
            wide, wide, wide, wide, box, box, box, box,
            pltpu.VMEM((4, LP, NX), F32),
            pltpu.VMEM((4, YE, NX), F32),
            pltpu.VMEM((4, YE, NX), F32),
            pltpu.VMEM((5, YE, NX), F32),
            pltpu.VMEM((5, YE, NX), F32),
            pltpu.SemaphoreType.DMA((8,)),
            pltpu.SemaphoreType.DMA((8,)),
        ],
        compiler_params=pltpu.CompilerParams(
            collective_id=1, has_side_effects=True, vmem_limit_bytes=48 << 20
        ),
        name="spread",
    )(field, coefs, row_halo, col_halo, corner)


def solve_body(matrix_ref, field_ref, out_ref):
    matrix = matrix_ref[pl.ds(0, LP), pl.ds(0, LP)]

    def row(y, _):
        product = jnp.dot(matrix, field_ref[y], precision=HI, preferred_element_type=F32)
        out_ref[pl.ds(y, LEV, stride=NY), :] = product[:LEV]
        return 0

    lax.fori_loop(0, NY, row, 0, unroll=2)


def solve_columns(matrix, field):
    vm = pl.BlockSpec(memory_space=pltpu.VMEM)
    return pl.pallas_call(
        solve_body,
        out_shape=jax.ShapeDtypeStruct((LEV * NY, NX), F32),
        in_specs=[vm, vm],
        out_specs=vm,
        compiler_params=pltpu.CompilerParams(vmem_limit_bytes=32 << 20),
        name="solve_columns",
    )(matrix, field)


def local(
    forcing, obs_values, obs_owner, obs_cell, obs_count,
    coef_east, coef_north, area_inv, sea_mask, vert_coef, inv_thick,
):
    matrix = vertical_fourth(vert_coef, inv_thick)
    coefs = jnp.stack([coef_east, coef_north, area_inv, sea_mask.astype(F32)])
    idx = places(obs_owner, obs_count)
    recv, row_halo, col_halo, corner = send_profiles(idx, obs_values, obs_cell, coefs)
    field = add_profiles(recv, forcing)
    field = spread(field, coefs, row_halo, col_halo, corner)
    return solve_columns(matrix, field).reshape(LEV, NY, NX)


def solution(mesh):
    lead = P(("lon", "lat"))
    flat = P("lat", "lon")
    in_specs = (
        P(None, "lat", "lon"), P(None, ("lon", "lat")), lead, lead, lead,
        flat, flat, flat, flat, P(), P(),
    )
    return jax.shard_map(
        local, mesh=mesh, in_specs=in_specs, out_specs=P(None, "lat", "lon"), check_vma=False
    )
```

time: 638 us -> 164 us (0.26)
  other arithmetic: 195 us -> 1.56 us
  Pallas kernels: 0 us -> 153 us
  local copies, waits for them, and re-layouts: 155 us -> 7.42 us
  loops' own time: 120 us -> 0 us
  waiting for transfers between devices: 68.9 us -> 0 us
  starting transfers between devices: 56 us -> 0 us
  between operations: 20.5 us -> 0.7 us
  matrix products: 15.8 us -> 0 us
    pallas_call x0 -> x6, Pallas kernels: none -> 153 us  [the longest x1 51.2 us: send_profiles(): pl.pallas_call(send_body, out_shape=(jax.ShapeDtypeStruct((DEV, ROWS, NX)...]
    another operation x3 -> x0, loops' own time: 120 us -> none  [the longest x2 120 us: vertical_inverse(): return lax.linalg.tridiagonal_solve(below, middle, above, ident)]
    scatter-add x1 -> x0, other arithmetic: 52.2 us -> none  [local(): adjoint = forcing.reshape(levels, rows_dev * cols_dev).at[:, got_cells[0]...]
    slice x40 -> x0, local copies, waits for them, and re-layouts: 48.3 us -> none  [the longest x9 23 us: padded_2(): last = lax.slice_in_dim(x, length - width, length, axis=dim)]
    div x4 -> x0, other arithmetic: 47.1 us -> none  [vertical_inverse(): return lax.linalg.tridiagonal_solve(below, middle, above, ident)]
    all_to_all x2 -> x0, waiting for transfers between devices: 45.7 us -> none  [the longest x1 45.7 us: local(): lax.all_to_all(send_values, ('lon', 'lat'), split_axis=1, concat_axis=1,...]
    sub x3 -> x0, other arithmetic: 42.3 us -> none  [the longest x2 40.4 us: vertical_inverse(): return lax.linalg.tridiagonal_solve(below, middle, above, ident)]
    ppermute x20 -> x0, starting transfers between devices: 37 us -> none  [the longest x10 24.2 us: padded_2(): before = lax.ppermute(last, axis, up)]
  transfers between devices with their start and end apart: 22 -> 0, of which waited for: 13 -> 0; matrix products, arithmetic and copies ran while one was open for 32% -> 0% of each run, Pallas kernels for 0% -> 0%
where the time goes in v1:
time: 164 us; the launch traced here: 163 us
  Pallas kernels  153 us (93%)
  local copies, waits for them, and re-layouts  7.42 us (5%)
    pallas_call x1, Pallas kernels, send_profiles(): pl.pallas_call(send_body, out_shape=(jax.ShapeDtypeStruct((DEV, ROWS, NX)...  51.2 us
    pallas_call x1, Pallas kernels, spread(): pl.pallas_call(spread_body, out_shape=jax.ShapeDtypeStruct((NY, LP, NX),...  47.5 us
    pallas_call x1, Pallas kernels, add_profiles(): pl.pallas_call(add_body, out_shape=jax.ShapeDtypeStruct((NY, LP, NX), F32...  33.8 us
    pallas_call x1, Pallas kernels, solve_columns(): pl.pallas_call(solve_body, out_shape=jax.ShapeDtypeStruct((LEV * NY, NX),...  10.1 us
    unnamed x12, local copies, waits for them, and re-layouts  7.42 us
    pallas_call x1, Pallas kernels, places(): pl.pallas_call(places_body, out_shape=jax.ShapeDtypeStruct((DEV, NX), jnp...  7.04 us
    pallas_call x1, Pallas kernels, vertical_fourth(): pl.pallas_call(vertical_body, out_shape=jax.ShapeDtypeStruct((NX, NX), F3...  3.42 us

profile of v1, /device:TPU:0, one launch (start us, length us, event | category | flops | bytes accessed | tf_op | source)
XLA Modules:
  0.0 162.7 jit_solution(10418588814598146659)
XLA Ops:
  0.0 0.8 convert_bitcast_fusion
  0.8 0.8 pad_maximum_fusion.coef_ref
  2.2 7.0 %places.1.idx_ref = s32[128,128]{1,0:T(8,128)} custom-call(s32[1]{0:T(128)S(6)} %copy.12.count_ref, s32[64,128]{1,0:T(8,128)} %bitcast.11), custom_call_target="tpu_custom_call" | custom-call | tf_op jit(solution)/shard_map/places/pallas_call | solution.py:107
  9.3 0.0 copy-start.1
  9.3 1.7 %copy-done.1 = f32[75,8192]{1,0:T(8,128)S(1)} copy-done((f32[75,8192]{1,0:T(8,128)S(1)}, f32[75,8192]{1,0:T(8,128)}, u32[]{:S(2)}) %copy-start.1) | copy-done | bytes 2457624
  11.0 0.0 copy-start.4
  11.0 0.8 copy-done.4
  11.8 0.0 copy-start.5
  11.8 0.8 copy-done.5
  12.6 51.2 %send_profiles.1 = (f32[128,40,128]{2,1,0:T(8,128)S(1)}, f32[2,4,8,128]{3,2,1,0:T(8,128)S(1)}, f32[2,64,128]{2,1,0:T(8,128)S(1)}, f32[4,8,128]{2,1,0:T(8,128)S(1)}) custom-call(s32[128,128]{1,0:T(8,128)S(1)} %copy-done.4, f32[75,8192]{1,0:T(8,128)S(1)} %copy-done.1, s32[64,128]{1,0:T(8,128)S(1)} %bitcast.9, f32[4,64,128]{2,1,0:T(8,128)S(1)} %pad_maximum_fusion.coef_ref), custom_call_target="tpu_custom_call" | custom-call | tf_op jit(solution)/shard_map/send_profiles/pallas_call | solution.py:233
  63.8 0.0 copy-start.2
  63.8 1.5 copy-done.2
  65.3 33.8 %add_profiles.1.field_ref = f32[64,80,128]{2,1,0:T(8,128)} custom-call(f32[128,40,128]{2,1,0:T(8,128)} %copy-done.2, f32[4800,128]{1,0:T(8,128)} %bitcast.10), custom_call_target="tpu_custom_call" | custom-call | tf_op jit(solution)/shard_map/add_profiles/pallas_call | solution.py:329
  99.1 0.0 copy-start
  99.1 1.7 %copy-done = f32[64,80,128]{2,1,0:T(8,128)S(1)} copy-done((f32[64,80,128]{2,1,0:T(8,128)S(1)}, f32[64,80,128]{2,1,0:T(8,128)}, u32[]{:S(2)}) %copy-start) | copy-done | bytes 2621464
  100.8 47.5 %spread.1.field_ref = f32[64,80,128]{2,1,0:T(8,128)S(1)} custom-call(f32[64,80,128]{2,1,0:T(8,128)S(1)} %copy-done, f32[4,64,128]{2,1,0:T(8,128)S(1)} %pad_maximum_fusion.coef_ref, f32[2,4,8,128]{3,2,1,0:T(8,128)S(1)} %get-tuple-element.10.row_halo_ref, f32[2,64,128]{2,1,0:T(8,128)S(1)} %get-tuple-element.11.col_halo_ref, ...), custom_call_target="tpu_custom_call" | custom-call | tf_op jit(solution)/shard_map/spread/pallas_call | solution.py:534
  148.3 3.4 %vertical.1.matrix_ref = f32[128,128]{1,0:T(8,128)} custom-call(f32[74]{0:T(128)} %vert_ref.1, f32[75]{0:T(128)} %thick_ref.1), custom_call_target="tpu_custom_call" | custom-call | tf_op jit(solution)/shard_map/vertical/pallas_call | solution.py:62
  151.7 0.0 copy-start.3
  151.7 0.8 copy-done.3
  152.5 10.1 %solve_columns.1 = f32[4800,128]{1,0:T(8,128)} custom-call(f32[128,128]{1,0:T(8,128)S(1)} %copy-done.3, f32[64,80,128]{2,1,0:T(8,128)S(1)} %spread.1.field_ref), custom_call_target="tpu_custom_call" | custom-call | tf_op jit(solution)/shard_map/solve_columns/pallas_call | solution.py:569
Async XLA Ops:
  9.3 1.7 %copy-start.1 = (f32[75,8192]{1,0:T(8,128)S(1)}, f32[75,8192]{1,0:T(8,128)}, u32[]{:S(2)}) copy-start(f32[75,8192]{1,0:T(8,128)} %obs_ref.1) | copy-start | bytes 7372804
  11.0 0.8 copy-start.4
  11.8 0.8 copy-start.5
  63.8 1.5 copy-start.2
  99.1 1.7 %copy-start = (f32[64,80,128]{2,1,0:T(8,128)S(1)}, f32[64,80,128]{2,1,0:T(8,128)}, u32[]{:S(2)}) copy-start(f32[64,80,128]{2,1,0:T(8,128)} %add_profiles.1.field_ref) | copy-start | bytes 7864324
  151.7 0.8 copy-start.3

commit v2 on v1

v2 whole, which is shorter than its diff:
```python
import jax
import jax.numpy as jnp
from jax import lax
from jax.experimental import pallas as pl
from jax.experimental.pallas import tpu as pltpu
from jax.sharding import PartitionSpec as P

LEV = 75
LP = 80
NX = 128
NY = 64
DEV = 128
CAP = 64
SLOTS = 8192
ROWS = 40
HALO = 4
YE = NY + 2 * HALO
Q = 18
STRIDE = 27
F32 = jnp.float32
BF16 = jnp.bfloat16
HI = lax.Precision.HIGHEST
MESH = pl.DeviceIdType.MESH


def iota(shape, dim, dtype=jnp.int32):
    return lax.broadcasted_iota(dtype, shape, dim)


def vertical_fourth(vert_ref, thick_ref, out_ref, cp_ref, dp_ref):
    lane = iota((1, NX), 1)
    dp_ref[...] = jnp.zeros_like(dp_ref)

    def forward(i, carry):
        cp, dp = carry
        up = jnp.where(i < LEV - 1, vert_ref[jnp.minimum(i, LEV - 2)], 0.0)
        low = jnp.where(i > 0, vert_ref[jnp.maximum(i - 1, 0)], 0.0)
        middle = 1.0 + (low + up) * thick_ref[i]
        above = -thick_ref[jnp.minimum(i + 1, LEV - 1)] * up
        below = -thick_ref[jnp.maximum(i - 1, 0)] * low
        inv = 1.0 / (middle - below * cp)
        cp = above * inv
        dp = (jnp.where(lane == i, 1.0, 0.0) - below * dp) * inv
        cp_ref[pl.ds(i, 1), :] = cp
        dp_ref[pl.ds(i, 1), :] = dp
        return cp, dp

    zero = jnp.zeros((1, NX), F32)
    lax.fori_loop(0, LEV, forward, (zero, zero))

    def backward(j, x):
        i = LEV - 1 - j
        x = dp_ref[pl.ds(i, 1), :] - cp_ref[pl.ds(i, 1), :] * x
        dp_ref[pl.ds(i, 1), :] = x
        return x

    lax.fori_loop(0, LEV, backward, zero)
    single = dp_ref[...]
    double = jnp.dot(single, single, precision=HI, preferred_element_type=F32)
    out_ref[...] = jnp.dot(double, double, precision=HI, preferred_element_type=F32)


def places(count, own_ref, idx_ref):
    width = 256
    lane = iota((1, width), 1)
    owners = iota((DEV, width), 0)
    tri = (iota((width, width + NX), 0) <= iota((width, width + NX), 1)) | (
        iota((width, width + NX), 1) >= width
    )
    tri = tri.astype(F32).astype(BF16)
    kth = iota((CAP, width), 0).astype(F32)
    number = (iota((CAP, width), 1) + 1).astype(F32)
    acc_lane = iota((DEV, NX), 1)

    def step(b, carry):
        offset, acc = carry
        own = jnp.concatenate([own_ref[pl.ds(2 * b, 1), :], own_ref[pl.ds(2 * b + 1, 1), :]], 1)
        own = jnp.where(lane + b * width < count, own, -1)
        onehot = jnp.where(jnp.broadcast_to(own, (DEV, width)) == owners, 1.0, 0.0)
        ones = onehot.astype(BF16)
        prefix = jnp.dot(ones, tri, preferred_element_type=F32)
        rank = prefix[:, :width] + jnp.concatenate([offset, offset], 1)
        rank = jnp.sum(onehot * rank, axis=0, keepdims=True) - 1.0
        hit = jnp.where(jnp.broadcast_to(rank, (CAP, width)) == kth, 1.0, 0.0)
        both = jnp.concatenate([hit, hit * number], 0).astype(BF16)
        found = lax.dot_general(ones, both, (((1,), (1,)), ((), ())), preferred_element_type=F32)
        scale = jnp.where(acc_lane < CAP, (b * width).astype(F32), 1.0)
        return offset + prefix[:, width:], acc + found * scale

    zero = jnp.zeros((DEV, NX), F32)
    _, acc = lax.fori_loop(0, SLOTS // width, step, (zero, zero), unroll=4)
    total = (acc + pltpu.roll(acc, CAP, 1)).astype(jnp.int32)
    idx_ref[...] = jnp.clip(jnp.where(total > 0, total - 1, SLOTS), 0, SLOTS)


def factors(coef_refs, row_halo_ref, col_halo_ref, corner_ref, coef_main, coef_side, fac_main_ref, fac_strip_ref):
    lat = lax.axis_index("lat")
    lane64 = iota((NY, NX), 1)
    lane4 = iota((HALO, NX), 1)
    for i in range(4):
        coef_main[i, pl.ds(HALO, NY), :] = coef_refs[i][...].astype(F32)
        coef_main[i, pl.ds(0, HALO), :] = row_halo_ref[0, i, pl.ds(4, HALO), :]
        coef_main[i, pl.ds(NY + HALO, HALO), :] = row_halo_ref[1, i, pl.ds(0, HALO), :]

        def sides(lanes, left, right, i=i):
            return jnp.where(
                lanes < 64,
                pltpu.roll(right, (-8 * i) % NX, 1),
                pltpu.roll(left, (124 - 8 * i - 4) % NX, 1),
            )

        coef_side[i, pl.ds(HALO, NY), :] = sides(lane64, col_halo_ref[0], col_halo_ref[1])
        coef_side[i, pl.ds(0, HALO), :] = sides(
            lane4, corner_ref[0, pl.ds(4, HALO), :], corner_ref[1, pl.ds(4, HALO), :]
        )
        coef_side[i, pl.ds(NY + HALO, HALO), :] = sides(
            lane4, corner_ref[2, pl.ds(0, HALO), :], corner_ref[3, pl.ds(0, HALO), :]
        )
    row = iota((YE, NX), 0)
    first_row = jnp.where(lat == 0, HALO, 0)
    last_row = jnp.where(lat == 3, NY + HALO, YE)
    inside = (row >= first_row) & (row < last_row)
    lanes = iota((YE, NX), 1)

    def shifts(main, side):
        first, last = lanes == 0, lanes == NX - 1
        main_e = pltpu.roll(jnp.where(first, side, main), NX - 1, 1)
        side_e = pltpu.roll(jnp.where(first, main, side), NX - 1, 1)
        main_w = pltpu.roll(jnp.where(last, side, main), 1, 1)
        side_w = pltpu.roll(jnp.where(last, main, side), 1, 1)
        return main_e, side_e, main_w, side_w

    sea_m = jnp.where(inside, coef_main[3], 0.0)
    sea_s = jnp.where(inside, coef_side[3], 0.0)
    area_m, area_s = coef_main[2], coef_side[2]
    sea_me, sea_se, _, _ = shifts(sea_m, sea_s)
    east_m = coef_main[0] * sea_m * sea_me
    east_s = coef_side[0] * sea_s * sea_se
    _, _, west_m, west_s = shifts(east_m, east_s)
    area_me, area_se, area_mw, area_sw = shifts(area_m, area_s)

    def five(north_coef, ee, ww, sea, area, area_e, area_w):
        nn = north_coef * sea * pltpu.roll(sea, YE - 1, 0)
        ss = pltpu.roll(nn, 1, 0)
        return (
            1.0 - area * (ee + ww + nn + ss),
            ee * area_e,
            ww * area_w,
            nn * pltpu.roll(area, YE - 1, 0),
            ss * pltpu.roll(area, 1, 0),
        )

    mains = five(coef_main[1], east_m, west_m, sea_m, area_m, area_me, area_mw)
    sides = five(coef_side[1], east_s, west_s, sea_s, area_s, area_se, area_sw)
    laneq = iota((Q, NX), 1)
    group, place = laneq // 32, laneq % 32
    gap = ((place >= 12) & (place < 16)) | (place >= 28)
    for i in range(5):
        fac_main_ref[i] = mains[i]
        coef_main[0] = jnp.where(lanes < 64, sides[i], mains[i])
        coef_main[1] = jnp.where(lanes < 64, mains[i], sides[i])
        strip = jnp.zeros((Q, NX), F32)
        for j in range(4):
            own = pl.ds(Q * j, Q)
            near = pltpu.roll(coef_main[0, own, :], (32 * j + 8) % NX, 1)
            far = pltpu.roll(coef_main[1, own, :], (32 * j + 20) % NX, 1)
            strip = jnp.where(group == j, jnp.where(place < 14, near, far), strip)
        fac_strip_ref[i, pl.ds(0, Q), :] = jnp.where(gap, 0.0, strip)


def send_body(
    count_ref, vert_ref, thick_ref, own_ref, obs_ref, cell_ref, east_ref, north_ref, area_ref, sea_ref,
    recv_ref, fac_main_ref, fac_strip_ref, matrix_ref,
    table, rows, outbox, coef_box, colbox, row_halo, col_halo, corner, coef_main, coef_side,
    cp_ref, dp_ref, idx_v, idx_ref, idx_sem, send_sem, recv_sem, side_send, side_recv,
):
    lon = lax.axis_index("lon")
    lat = lax.axis_index("lat")
    z, y, c = lax.div(lon, 8), lax.rem(lax.div(lon, 2), 4), lax.rem(lon, 2)
    me = lon * 4 + lat

    def target(k):
        q = lax.rem(k * STRIDE, DEV)
        dx, dc = lax.rem(q, 4), lax.rem(lax.div(q, 4), 2)
        dy, dz = lax.rem(lax.div(q, 8), 4), lax.div(q, 32)
        there = (lax.rem(z + dz, 4) * 4 + lax.rem(y + dy, 4)) * 2 + lax.rem(c + dc, 2)
        return there, lax.rem(lat + dx, 4)

    barrier = pltpu.get_barrier_semaphore()

    def greet(k, _):
        pl.semaphore_signal(barrier, inc=1, device_id=target(k), device_id_type=MESH)
        return 0

    lax.fori_loop(1, DEV, greet, 0)

    places(count_ref[0], own_ref, idx_v)
    idx_copy = pltpu.make_async_copy(idx_v, idx_ref, idx_sem)
    idx_copy.start()

    def turn(b, _):
        columns = pl.ds(pl.multiple_of(b * NX, NX), NX)
        block = jnp.concatenate(
            [
                obs_ref[:, columns],
                cell_ref[pl.ds(b, 1), :].astype(F32),
                jnp.zeros((NX - LEV - 1, NX), F32),
            ],
            0,
        )
        table[columns, :] = block.T
        return 0

    lax.fori_loop(0, SLOTS // NX, turn, 0, unroll=4)
    table[pl.ds(SLOTS, 8), :] = jnp.zeros((8, NX), F32)

    lane = iota((NY, NX), 1)
    cols = jnp.zeros((NY, NX), F32)
    coef_refs = (east_ref, north_ref, area_ref, sea_ref)
    for i in range(4):
        whole = coef_refs[i][...].astype(F32)
        coef_box[i, pl.ds(0, 8), :] = whole[:8]
        coef_box[i, pl.ds(8, 8), :] = whole[NY - 8:]
        cols = jnp.where((lane >= 8 * i) & (lane < 8 * i + 4), pltpu.roll(whole, 8 * i, 1), cols)
        cols = jnp.where(
            (lane >= 8 * i + 4) & (lane < 8 * i + 8),
            pltpu.roll(whole, (8 * i + 4 - 124) % NX, 1),
            cols,
        )
    colbox[...] = cols
    idx_copy.wait()
    pl.semaphore_wait(barrier, DEV - 1)

    east, west = lax.rem(lon + 1, 32), lax.rem(lon + 31, 32)
    north, south = lax.rem(lat + 1, 4), lax.rem(lat + 3, 4)
    side = []

    def beside(number, src, dst, where):
        copy = pltpu.make_async_remote_copy(
            src_ref=src, dst_ref=dst, send_sem=side_send.at[number], recv_sem=side_recv.at[number],
            device_id=where, device_id_type=MESH,
        )
        copy.start()
        side.append(copy)

    beside(0, coef_box.at[:, pl.ds(8, 8), :], row_halo.at[0], (lon, north))
    beside(1, coef_box.at[:, pl.ds(0, 8), :], row_halo.at[1], (lon, south))
    beside(2, colbox, col_halo.at[0], (east, lat))
    beside(3, colbox, col_halo.at[1], (west, lat))
    beside(4, colbox.at[pl.ds(NY - 8, 8), :], corner.at[0], (east, north))
    beside(5, colbox.at[pl.ds(NY - 8, 8), :], corner.at[1], (west, north))
    beside(6, colbox.at[pl.ds(0, 8), :], corner.at[2], (east, south))
    beside(7, colbox.at[pl.ds(0, 8), :], corner.at[3], (west, south))

    lane8 = iota((8, NX), 1)
    lane32 = iota((32, NX), 1)

    def gather(owner):
        for k in range(CAP):
            at = jnp.minimum(jnp.maximum(idx_ref[owner, k], 0), SLOTS)
            rows[pl.ds(k, 1), :] = table[pl.ds(at, 1), :]

    def fold(box):
        box[pl.ds(0, 32), :] = jnp.where(
            lane32 < 64, rows[pl.ds(0, 32), :], pltpu.roll(rows[pl.ds(32, 32), :], 64, 1)
        )
        rest = jnp.zeros((8, NX), F32)
        for g in range(8):
            piece = rows[pl.ds(8 * g, 8), :]
            shift = (16 * g - 64) % NX
            piece = pltpu.roll(piece, shift, 1) if shift else piece
            rest = jnp.where(lane8 // 16 == g, piece, rest)
        box[pl.ds(32, 8), :] = rest

    def send(k, _):
        dlon, dlat = target(k)
        owner = dlon * 4 + dlat
        gather(owner)
        fold(outbox.at[owner])
        pltpu.make_async_remote_copy(
            src_ref=outbox.at[owner], dst_ref=recv_ref.at[me], send_sem=send_sem, recv_sem=recv_sem,
            device_id=(dlon, dlat), device_id_type=MESH,
        ).start()
        return 0

    lax.fori_loop(1, DEV, send, 0)
    gather(me)
    fold(recv_ref.at[me])
    vertical_fourth(vert_ref, thick_ref, matrix_ref, cp_ref, dp_ref)
    for copy in side:
        copy.wait()
    factors(coef_refs, row_halo, col_halo, corner, coef_main, coef_side, fac_main_ref, fac_strip_ref)
    others = pl.ds(0, DEV - 1)
    pltpu.make_async_copy(outbox.at[others], outbox.at[others], send_sem).wait()
    pltpu.make_async_copy(recv_ref.at[others], recv_ref.at[others], recv_sem).wait()


def send_profiles(count, vert_coef, inv_thick, owner, obs, cell, coefs):
    vm = pl.BlockSpec(memory_space=pltpu.VMEM)
    sm = pl.BlockSpec(memory_space=pltpu.SMEM)
    plane = pltpu.VMEM((4, YE, NX), F32)
    return pl.pallas_call(
        send_body,
        out_shape=(
            jax.ShapeDtypeStruct((DEV, ROWS, NX), F32),
            jax.ShapeDtypeStruct((5, YE, NX), F32),
            jax.ShapeDtypeStruct((5, 24, NX), F32),
            jax.ShapeDtypeStruct((NX, NX), F32),
        ),
        in_specs=[sm] * 3 + [vm] * 7,
        out_specs=(vm,) * 4,
        scratch_shapes=[
            pltpu.VMEM((SLOTS + 8, NX), F32),
            pltpu.VMEM((CAP, NX), F32),
            pltpu.VMEM((DEV, ROWS, NX), F32),
            pltpu.VMEM((4, 16, NX), F32),
            pltpu.VMEM((NY, NX), F32),
            pltpu.VMEM((2, 4, 8, NX), F32),
            pltpu.VMEM((2, NY, NX), F32),
            pltpu.VMEM((4, 8, NX), F32),
            plane,
            plane,
            pltpu.VMEM((NX, NX), F32),
            pltpu.VMEM((NX, NX), F32),
            pltpu.VMEM((DEV, NX), jnp.int32),
            pltpu.SMEM((DEV, NX), jnp.int32),
            pltpu.SemaphoreType.DMA(()),
            pltpu.SemaphoreType.DMA(()),
            pltpu.SemaphoreType.DMA(()),
            pltpu.SemaphoreType.DMA((8,)),
            pltpu.SemaphoreType.DMA((8,)),
        ],
        compiler_params=pltpu.CompilerParams(
            collective_id=0, has_side_effects=True, vmem_limit_bytes=48 << 20
        ),
        name="send_profiles",
    )(
        count, vert_coef, inv_thick, owner.reshape(SLOTS // NX, NX), obs,
        cell.reshape(SLOTS // NX, NX), *coefs,
    )


WAYS = 4


def add_body(recv_ref, forcing_ref, matrix_ref, out_ref, full, acc0, acc1, acc2, acc3, cell_v, cell_s, sem):
    accs = (acc0, acc1, acc2, acc3)
    pick = jnp.where(
        iota((8, NX), 1) == 16 * iota((8, NX), 0) + (LEV - 64), 1.0, 0.0
    ).astype(F32)

    def cells(b, _):
        part = recv_ref[pl.ds(16 * b, 16), pl.ds(32, 8), :].reshape(NX, NX)
        found = lax.dot_general(
            pick, part, (((1,), (1,)), ((), ())), precision=HI, preferred_element_type=F32
        )
        cell_v[:, pl.ds(pl.multiple_of(b * NX, NX), NX)] = (found + 0.5).astype(jnp.int32)
        return 0

    lax.fori_loop(0, 8, cells, 0, unroll=True)
    copy = pltpu.make_async_copy(cell_v, cell_s, sem)
    copy.start()

    def unfold(s, _):
        rest = recv_ref[s, pl.ds(32, 8), :]
        lane8 = iota((8, NX), 1)
        for g in range(8):
            tail = pltpu.roll(rest, (64 - 16 * g) % NX, 1) if g != 4 else rest
            head = recv_ref[s, pl.ds(8 * (g % 4), 8), :]
            head = pltpu.roll(head, 64, 1) if g >= 4 else head
            full[pl.ds(s * CAP + 8 * g, 8), :] = jnp.where(lane8 < 64, head, tail)
        return 0

    lax.fori_loop(0, DEV, unfold, 0, unroll=4)

    def clear(i, _):
        at = pl.ds(pl.multiple_of(i * 64, 64), 64)
        for acc in accs:
            acc[at, :] = jnp.zeros((64, NX), F32)
        return 0

    lax.fori_loop(0, SLOTS // 64, clear, 0, unroll=2)
    copy.wait()
    per = DEV // WAYS

    def add(s, _):
        for g in range(8):
            for e in range(8):
                for w, acc in enumerate(accs):
                    src = s + w * per
                    cell = cell_s[g, src * 8 + e]
                    at = pl.ds(cell, 1)
                    acc[at, :] = acc[at, :] + full[pl.ds(src * CAP + 8 * g + e, 1), :]
        return 0

    lax.fori_loop(0, per, add, 0)

    matrix = matrix_ref[pl.ds(0, LP), pl.ds(0, LEV)]

    def finish(b, _):
        loaded = []
        for h in range(2):
            y = 2 * b + h
            at = pl.ds(pl.multiple_of(y * NX, NX), NX)
            total = (acc0[at, :] + acc1[at, :]) + (acc2[at, :] + acc3[at, :])
            loaded.append(total.T[:LEV] + forcing_ref[pl.ds(y, LEV, stride=NY), :])
        product = jnp.dot(
            matrix, jnp.concatenate(loaded, 1), precision=HI, preferred_element_type=F32
        )
        out_ref[2 * b] = product[:, :NX]
        out_ref[2 * b + 1] = product[:, NX:]
        return 0

    lax.fori_loop(0, NY // 2, finish, 0, unroll=4)


def add_profiles(recv, forcing, matrix):
    vm = pl.BlockSpec(memory_space=pltpu.VMEM)
    return pl.pallas_call(
        add_body,
        out_shape=jax.ShapeDtypeStruct((NY, LP, NX), F32),
        in_specs=[vm, vm, vm],
        out_specs=vm,
        scratch_shapes=[pltpu.VMEM((SLOTS, NX), F32)] * 5
        + [
            pltpu.VMEM((8, 8 * DEV), jnp.int32),
            pltpu.SMEM((8, 8 * DEV), jnp.int32),
            pltpu.SemaphoreType.DMA(()),
        ],
        compiler_params=pltpu.CompilerParams(vmem_limit_bytes=56 << 20),
        name="add_profiles",
    )(recv, forcing.reshape(LEV * NY, NX), matrix)


def spread_body(
    field_ref, fac_ref, strip_ref,
    out_ref,
    wide_a, wide_b, tips, strip_a, strip_b, east_box, west_box, from_west, from_east, corners,
    own_sem, send_sem, recv_sem,
):
    lon = lax.axis_index("lon")
    lat = lax.axis_index("lat")
    east, west = lax.rem(lon + 1, 32), lax.rem(lon + 31, 32)
    north, south = lax.rem(lat + 1, 4), lax.rem(lat + 3, 4)
    peers = [
        (lon, north), (lon, south), (east, lat), (west, lat),
        (east, north), (west, north), (east, south), (west, south),
    ]
    barrier = pltpu.get_barrier_semaphore()
    for peer in peers:
        pl.semaphore_signal(barrier, inc=1, device_id=peer, device_id_type=MESH)
    own = pltpu.make_async_copy(field_ref, wide_a.at[pl.ds(HALO, NY)], own_sem)
    own.start()
    own.wait()

    lane = iota((LP, NX), 1)
    group, place = lane // 32, lane % 32

    def tip(low, high, parts):
        def one(q, _):
            total = jnp.zeros((LP, NX), F32)
            for j in parts:
                piece = pltpu.roll(wide_a[q + Q * j], (32 * j + 8) % NX, 1)
                total = jnp.where((group == j) & (place < 16), piece, total)
            tips[q] = total
            return 0

        lax.fori_loop(low, high, one, 0, unroll=2)

    tip(0, HALO, (1, 2, 3))
    tip(HALO, Q - HALO, (0, 1, 2, 3))
    tip(Q - HALO, Q, (0, 1, 2))
    for b in range(3):
        e = jnp.zeros((LP, NX), F32)
        w = jnp.zeros((LP, NX), F32)
        for q in range(8 * b, min(8 * b + 8, Q)):
            here = place // 4 == q % 8
            row = tips[q]
            e = jnp.where(here, pltpu.roll(row, (4 * (q % 8) - 4) % NX, 1), e)
            w = jnp.where(here, pltpu.roll(row, (4 * (q % 8) - 8) % NX, 1), w)
        east_box[b] = e
        west_box[b] = w

    pl.semaphore_wait(barrier, 8)
    moves = [
        (field_ref.at[pl.ds(NY - HALO, HALO)], wide_a.at[pl.ds(0, HALO)]),
        (field_ref.at[pl.ds(0, HALO)], wide_a.at[pl.ds(NY + HALO, HALO)]),
        (east_box, from_west),
        (west_box, from_east),
        (east_box.at[1], corners.at[0]),
        (west_box.at[1], corners.at[1]),
        (east_box.at[0], corners.at[2]),
        (west_box.at[0], corners.at[3]),
    ]
    copies = []
    for number, (src, dst) in enumerate(moves):
        copy = pltpu.make_async_remote_copy(
            src_ref=src, dst_ref=dst, send_sem=send_sem.at[number], recv_sem=recv_sem.at[number],
            device_id=peers[number], device_id_type=MESH,
        )
        copy.start()
        copies.append(copy)

    def stencil(facs, y, src, at):
        centre = src[at]

        def fac(i):
            return jnp.broadcast_to(facs[i, pl.ds(y, 1), :], (LP, NX))

        return (
            fac(0) * centre
            + fac(1) * pltpu.roll(centre, NX - 1, 1)
            + fac(2) * pltpu.roll(centre, 1, 1)
            + fac(3) * src[at + 1]
            + fac(4) * src[at - 1]
        )

    def rows(t, low, high, unroll):
        src, dst = (wide_a, wide_b) if t % 2 else (wide_b, wide_a)

        def row(y, _):
            dst[y] = stencil(fac_ref, y, src, y)
            return 0

        lax.fori_loop(low, high, row, 0, unroll=unroll)

    for t in range(1, 5):
        rows(t, HALO + t, NY + HALO - t, 8)

    for copy in copies:
        copy.wait()

    for near, from_side in ((0, from_west), (1, from_east)):
        below, above = corners[near], corners[near + 2]
        from_side[0] = jnp.where(lane < 16, pltpu.roll(below, 24, 1), from_side[0])
        from_side[1] = jnp.where(lane >= 120, pltpu.roll(above, 104, 1), from_side[1])
        from_side[2] = jnp.where((lane >= 96) & (lane < 104), pltpu.roll(above, 72, 1), from_side[2])
    for h in range(HALO):
        q = Q - HALO + h
        tips[h] = jnp.where((group == 0) & (place < 16), pltpu.roll(wide_a[h], 8, 1), tips[h])
        tips[q] = jnp.where((group == 3) & (place < 16), pltpu.roll(wide_a[q + 3 * Q], 104, 1), tips[q])
    for q in range(Q):
        row = tips[q]
        right = pltpu.roll(from_east[q // 8], (8 - 4 * (q % 8)) % NX, 1)
        left = pltpu.roll(from_west[q // 8], (16 - 4 * (q % 8)) % NX, 1)
        far = jnp.where((place >= 16) & (place < 20), left, pltpu.roll(row, 12, 1))
        strip_a[q + 1] = jnp.where(place < 8, row, jnp.where(place < 12, right, far))

    for t in range(1, 5):
        rows(t, t, HALO + t, 4)
        rows(t, NY + HALO - t, NY + 2 * HALO - t, 4)
    for t in range(4):
        src, dst = (strip_a, strip_b) if t % 2 == 0 else (strip_b, strip_a)
        src[0] = pltpu.roll(src[Q], 32, 1)
        src[Q + 1] = pltpu.roll(src[1], NX - 32, 1)

        def strip(q, _):
            dst[q + 1] = stencil(strip_ref, q, src, q + 1)
            return 0

        lax.fori_loop(0, Q, strip, 0, unroll=6)

    edge = (lane < HALO) | (lane >= NX - HALO)

    def write(low, high, parts):
        def one(q, _):
            row = strip_a[q + 1]
            row = jnp.where(place < 8, row, pltpu.roll(row, NX - 12, 1))
            for j in parts:
                y = q + Q * j
                whole = jnp.where(edge, pltpu.roll(row, (120 - 32 * j) % NX, 1), wide_a[y])
                out_ref[pl.ds(y - HALO, LEV, stride=NY), :] = whole[:LEV]
            return 0

        lax.fori_loop(low, high, one, 0, unroll=2)

    write(0, HALO, (1, 2, 3))
    write(HALO, Q - HALO, (0, 1, 2, 3))
    write(Q - HALO, Q, (0, 1, 2))


def spread(field, fac_main, fac_strip):
    vm = pl.BlockSpec(memory_space=pltpu.VMEM)
    wide = pltpu.VMEM((YE, LP, NX), F32)
    strip = pltpu.VMEM((Q + 2, LP, NX), F32)
    box = pltpu.VMEM((3, LP, NX), F32)
    return pl.pallas_call(
        spread_body,
        out_shape=jax.ShapeDtypeStruct((LEV * NY, NX), F32),
        in_specs=[pl.BlockSpec(memory_space=pl.ANY), vm, vm],
        out_specs=vm,
        scratch_shapes=[
            wide, wide, pltpu.VMEM((Q, LP, NX), F32), strip, strip, box, box, box, box,
            pltpu.VMEM((4, LP, NX), F32),
            pltpu.SemaphoreType.DMA(()),
            pltpu.SemaphoreType.DMA((8,)),
            pltpu.SemaphoreType.DMA((8,)),
        ],
        compiler_params=pltpu.CompilerParams(
            collective_id=1, has_side_effects=True, vmem_limit_bytes=40 << 20
        ),
        name="spread",
    )(field, fac_main, fac_strip)


def local(
    forcing, obs_values, obs_owner, obs_cell, obs_count,
    coef_east, coef_north, area_inv, sea_mask, vert_coef, inv_thick,
):
    coefs = (coef_east, coef_north, area_inv, sea_mask)
    recv, fac_main, fac_strip, matrix = send_profiles(
        obs_count, vert_coef, inv_thick, obs_owner, obs_values, obs_cell, coefs
    )
    field = add_profiles(recv, forcing, matrix)
    return spread(field, fac_main, fac_strip).reshape(LEV, NY, NX)


def solution(mesh):
    lead = P(("lon", "lat"))
    flat = P("lat", "lon")
    in_specs = (
        P(None, "lat", "lon"), P(None, ("lon", "lat")), lead, lead, lead,
        flat, flat, flat, flat, P(), P(),
    )
    return jax.shard_map(
        local, mesh=mesh, in_specs=in_specs, out_specs=P(None, "lat", "lon"), check_vma=False
    )
```

time: 164 us -> 115 us (0.70)
  Pallas kernels: 153 us -> 100 us
  local copies, waits for them, and re-layouts: 7.42 us -> 12.9 us
    pallas_call x4 -> x1, Pallas kernels: 68.1 us -> 18.6 us  [spread(): pl.pallas_call(spread_body, out_shape=jax.ShapeDtypeStruct((LEV * NY, NX)...]
    unnamed x12 -> x25, local copies, waits for them, and re-layouts: 7.42 us -> 12.9 us
    pallas_call x1, Pallas kernels: 33.8 us -> 30.7 us  [add_profiles(): pl.pallas_call(add_body, out_shape=jax.ShapeDtypeStruct((NY, LP, NX), F32...]
where the time goes in v2:
time: 115 us; the launch traced here: 114 us
  Pallas kernels  100 us (87%)
  local copies, waits for them, and re-layouts  12.9 us (11%)
    pallas_call x1, Pallas kernels, send_profiles(): pl.pallas_call(send_body, out_shape=(jax.ShapeDtypeStruct((DEV, ROWS, NX)...  51.1 us
    pallas_call x1, Pallas kernels, add_profiles(): pl.pallas_call(add_body, out_shape=jax.ShapeDtypeStruct((NY, LP, NX), F32...  30.7 us
    pallas_call x1, Pallas kernels, spread(): pl.pallas_call(spread_body, out_shape=jax.ShapeDtypeStruct((LEV * NY, NX)...  18.6 us
    unnamed x25, local copies, waits for them, and re-layouts  12.9 us

profile of v2, /device:TPU:0, one launch (start us, length us, event | category | flops | bytes accessed | tf_op | source)
XLA Modules:
  0.0 113.9 jit_solution(7028394111050231130)
XLA Ops:
  0.7 0.0 copy-start.1
  0.7 1.7 %copy-done.1 = f32[75,8192]{1,0:T(8,128)S(1)} copy-done((f32[75,8192]{1,0:T(8,128)S(1)}, f32[75,8192]{1,0:T(8,128)}, u32[]{:S(2)}) %copy-start.1) | copy-done | bytes 2457624
  2.4 0.0 copy-start.4
  2.4 0.8 copy-done.4
  3.2 0.0 copy-start.5
  3.2 0.8 copy-done.5
  3.9 0.0 copy-start.6
  3.9 0.8 copy-done.6
  4.7 0.0 copy-start.7
  4.7 0.8 copy-done.7
  5.4 0.0 copy-start.8
  5.4 0.8 copy-done.8
  6.2 0.0 copy-start.9
  6.2 0.8 copy-done.9
  6.9 0.0 copy-start.10
  6.9 0.7 copy-done.10
  7.6 0.0 copy-start.11
  7.6 0.7 copy-done.11
  8.3 51.1 %send_profiles.1 = (f32[128,40,128]{2,1,0:T(8,128)S(1)}, f32[5,72,128]{2,1,0:T(8,128)S(1)}, f32[5,24,128]{2,1,0:T(8,128)S(1)}, f32[128,128]{1,0:T(8,128)S(1)}) custom-call(s32[1]{0:T(128)S(6)} %copy.13.count_ref, f32[74]{0:T(128)S(1)} %copy-done.10, f32[75]{0:T(128)S(1)} %copy-done.11, s32[64,128]{1,0:T(8,128)S(1)} %bitcast.5, f32[75,8192]{1,0:T(8,128)S(1)} %copy-done.1, ...), custom_call_target="tpu_custom_call" | custom-call | tf_op jit(solution)/shard_map/send_profiles/pallas_call | solution.py:302
  59.3 0.0 copy-start.2
  59.3 1.5 %copy-done.2 = f32[128,40,128]{2,1,0:T(8,128)} copy-done((f32[128,40,128]{2,1,0:T(8,128)}, f32[128,40,128]{2,1,0:T(8,128)S(1)}, u32[]{:S(2)}) %copy-start.2) | copy-done | bytes 2621464
  60.8 0.0 copy-start.3
  60.8 0.6 copy-done.3
  61.5 30.7 %add_profiles.1.field_ref = f32[64,80,128]{2,1,0:T(8,128)} custom-call(f32[128,40,128]{2,1,0:T(8,128)} %copy-done.2, f32[4800,128]{1,0:T(8,128)} %bitcast.7, f32[128,128]{1,0:T(8,128)} %copy-done.3), custom_call_target="tpu_custom_call" | custom-call | tf_op jit(solution)/shard_map/add_profiles/pallas_call | solution.py:419
  92.1 0.0 copy-start
  92.2 1.7 %copy-done = f32[64,80,128]{2,1,0:T(8,128)S(1)} copy-done((f32[64,80,128]{2,1,0:T(8,128)S(1)}, f32[64,80,128]{2,1,0:T(8,128)}, u32[]{:S(2)}) %copy-start) | copy-done | bytes 2621464
  93.9 18.6 %spread.1 = f32[4800,128]{1,0:T(8,128)S(1)} custom-call(f32[64,80,128]{2,1,0:T(8,128)S(1)} %copy-done, f32[5,72,128]{2,1,0:T(8,128)S(1)} %get-tuple-element.11.fac_ref, f32[5,24,128]{2,1,0:T(8,128)S(1)} %get-tuple-element.12.strip_ref), custom_call_target="tpu_custom_call" | custom-call | tf_op jit(solution)/shard_map/spread/pallas_call | solution.py:587
  112.5 1.4 %copy.14 = f32[75,64,128]{2,1,0:T(8,128)} copy(f32[75,64,128]{2,1,0:T(8,128)S(1)} %bitcast.4) | data formatting | bytes 4915200
Async XLA Ops:
  0.7 1.7 %copy-start.1 = (f32[75,8192]{1,0:T(8,128)S(1)}, f32[75,8192]{1,0:T(8,128)}, u32[]{:S(2)}) copy-start(f32[75,8192]{1,0:T(8,128)} %obs_ref.1) | copy-start | bytes 7372804
  2.4 0.8 copy-start.4
  3.2 0.8 copy-start.5
  3.9 0.8 copy-start.6
  4.7 0.8 copy-start.7
  5.4 0.8 copy-start.8
  6.2 0.8 copy-start.9
  6.9 0.7 copy-start.10
  7.6 0.7 copy-start.11
  59.3 1.5 %copy-start.2 = (f32[128,40,128]{2,1,0:T(8,128)}, f32[128,40,128]{2,1,0:T(8,128)S(1)}, u32[]{:S(2)}) copy-start(f32[128,40,128]{2,1,0:T(8,128)S(1)} %get-tuple-element.9.recv_ref) | copy-start | bytes 7864324
  60.8 0.6 copy-start.3
  92.1 1.7 %copy-start = (f32[64,80,128]{2,1,0:T(8,128)S(1)}, f32[64,80,128]{2,1,0:T(8,128)}, u32[]{:S(2)}) copy-start(f32[64,80,128]{2,1,0:T(8,128)} %add_profiles.1.field_ref) | copy-start | bytes 7864324

commit v3 on v2

--- a/solution.py
+++ b/solution.py
@@ -23,6 +23,10 @@
 MESH = pl.DeviceIdType.MESH
 
 
+def in_hbm(x):
+    return pltpu.with_memory_space_constraint(x, pltpu.HBM)
+
+
 def iota(shape, dim, dtype=jnp.int32):
     return lax.broadcasted_iota(dtype, shape, dim)
 
@@ -169,9 +173,10 @@
 
 
 def send_body(
-    count_ref, vert_ref, thick_ref, own_ref, obs_ref, cell_ref, east_ref, north_ref, area_ref, sea_ref,
-    recv_ref, fac_main_ref, fac_strip_ref, matrix_ref,
-    table, rows, outbox, coef_box, colbox, row_halo, col_halo, corner, coef_main, coef_side,
+    count_ref, vert_hbm, thick_hbm, own_hbm, obs_hbm, cell_hbm, east_hbm, north_hbm, area_hbm, sea_hbm,
+    full_ref, cells_ref, fac_main_ref, fac_strip_ref, matrix_ref,
+    vert_ref, thick_ref, own_ref, obs_ref, cell_ref, east_ref, north_ref, area_ref, sea_ref,
+    recv, load_sem, table, rows, outbox, coef_box, colbox, row_halo, col_halo, corner, coef_main, coef_side,
     cp_ref, dp_ref, idx_v, idx_ref, idx_sem, send_sem, recv_sem, side_send, side_recv,
 ):
     lon = lax.axis_index("lon")
@@ -186,6 +191,16 @@
         there = (lax.rem(z + dz, 4) * 4 + lax.rem(y + dy, 4)) * 2 + lax.rem(c + dc, 2)
         return there, lax.rem(lat + dx, 4)
 
+    loads = []
+    for number, (src, dst) in enumerate((
+        (own_hbm, own_ref), (obs_hbm, obs_ref), (cell_hbm, cell_ref), (east_hbm, east_ref),
+        (north_hbm, north_ref), (area_hbm, area_ref), (sea_hbm, sea_ref),
+        (vert_hbm, vert_ref), (thick_hbm, thick_ref),
+    )):
+        load = pltpu.make_async_copy(src, dst, load_sem.at[number])
+        load.start()
+        loads.append(load)
+
     barrier = pltpu.get_barrier_semaphore()
 
     def greet(k, _):
@@ -194,9 +209,12 @@
 
     lax.fori_loop(1, DEV, greet, 0)
 
+    loads[0].wait()
     places(count_ref[0], own_ref, idx_v)
     idx_copy = pltpu.make_async_copy(idx_v, idx_ref, idx_sem)
     idx_copy.start()
+    for load in loads[1:]:
+        load.wait()
 
     def turn(b, _):
         columns = pl.ds(pl.multiple_of(b * NX, NX), NX)
@@ -278,21 +296,48 @@
         gather(owner)
         fold(outbox.at[owner])
         pltpu.make_async_remote_copy(
-            src_ref=outbox.at[owner], dst_ref=recv_ref.at[me], send_sem=send_sem, recv_sem=recv_sem,
+            src_ref=outbox.at[owner], dst_ref=recv.at[k], send_sem=send_sem, recv_sem=recv_sem.at[k],
             device_id=(dlon, dlat), device_id_type=MESH,
         ).start()
         return 0
 
     lax.fori_loop(1, DEV, send, 0)
     gather(me)
-    fold(recv_ref.at[me])
+    fold(recv.at[0])
     vertical_fourth(vert_ref, thick_ref, matrix_ref, cp_ref, dp_ref)
     for copy in side:
         copy.wait()
     factors(coef_refs, row_halo, col_halo, corner, coef_main, coef_side, fac_main_ref, fac_strip_ref)
+    pick = jnp.where(
+        iota((8, NX), 1) == 16 * iota((8, NX), 0) + (LEV - 64), 1.0, 0.0
+    ).astype(F32)
+
+    def unfold(k):
+        rest = recv[k, pl.ds(32, 8), :]
+        for g in range(8):
+            tail = pltpu.roll(rest, (64 - 16 * g) % NX, 1) if g != 4 else rest
+            head = recv[k, pl.ds(8 * (g % 4), 8), :]
+            head = pltpu.roll(head, 64, 1) if g >= 4 else head
+            full_ref[pl.ds(k * CAP + 8 * g, 8), :] = jnp.where(lane8 < 64, head, tail)
+
+    def arrive(k, _):
+        pltpu.make_async_copy(recv.at[k], recv.at[k], recv_sem.at[k]).wait()
+        return 0
+
+    def spread_out(k, _):
+        unfold(k)
+        return 0
+
+    for b in range(8):
+        lax.fori_loop(max(16 * b, 1), 16 * b + 16, arrive, 0)
+        lax.fori_loop(16 * b, 16 * b + 16, spread_out, 0, unroll=4)
+        part = recv[pl.ds(16 * b, 16), pl.ds(32, 8), :].reshape(NX, NX)
+        found = lax.dot_general(
+            pick, part, (((1,), (1,)), ((), ())), precision=HI, preferred_element_type=F32
+        )
+        cells_ref[:, pl.ds(NX * b, NX)] = (found + 0.5).astype(jnp.int32)
     others = pl.ds(0, DEV - 1)
     pltpu.make_async_copy(outbox.at[others], outbox.at[others], send_sem).wait()
-    pltpu.make_async_copy(recv_ref.at[others], recv_ref.at[others], recv_sem).wait()
 
 
 def send_profiles(count, vert_coef, inv_thick, owner, obs, cell, coefs):
@@ -302,14 +347,26 @@
     return pl.pallas_call(
         send_body,
         out_shape=(
-            jax.ShapeDtypeStruct((DEV, ROWS, NX), F32),
+            jax.ShapeDtypeStruct((SLOTS, NX), F32),
+            jax.ShapeDtypeStruct((8, 8 * DEV), jnp.int32),
             jax.ShapeDtypeStruct((5, YE, NX), F32),
             jax.ShapeDtypeStruct((5, 24, NX), F32),
             jax.ShapeDtypeStruct((NX, NX), F32),
         ),
-        in_specs=[sm] * 3 + [vm] * 7,
-        out_specs=(vm,) * 4,
+        in_specs=[sm] + [pl.BlockSpec(memory_space=pltpu.HBM)] * 9,
+        out_specs=(vm,) * 5,
         scratch_shapes=[
+            pltpu.SMEM((LEV - 1,), F32),
+            pltpu.SMEM((LEV,), F32),
+            pltpu.VMEM((SLOTS // NX, NX), jnp.int32),
+            pltpu.VMEM((LEV, SLOTS), F32),
+            pltpu.VMEM((SLOTS // NX, NX), jnp.int32),
+            pltpu.VMEM((NY, NX), F32),
+            pltpu.VMEM((NY, NX), F32),
+            pltpu.VMEM((NY, NX), F32),
+            pltpu.VMEM((NY, NX), jnp.int32),
+            pltpu.VMEM((DEV, ROWS, NX), F32),
+            pltpu.SemaphoreType.DMA((9,)),
             pltpu.VMEM((SLOTS + 8, NX), F32),
             pltpu.VMEM((CAP, NX), F32),
             pltpu.VMEM((DEV, ROWS, NX), F32),
@@ -326,52 +383,27 @@
             pltpu.SMEM((DEV, NX), jnp.int32),
             pltpu.SemaphoreType.DMA(()),
             pltpu.SemaphoreType.DMA(()),
-            pltpu.SemaphoreType.DMA(()),
+            pltpu.SemaphoreType.DMA((DEV,)),
             pltpu.SemaphoreType.DMA((8,)),
             pltpu.SemaphoreType.DMA((8,)),
         ],
         compiler_params=pltpu.CompilerParams(
-            collective_id=0, has_side_effects=True, vmem_limit_bytes=48 << 20
+            collective_id=0, has_side_effects=True, vmem_limit_bytes=24 << 20
         ),
         name="send_profiles",
-    )(
-        count, vert_coef, inv_thick, owner.reshape(SLOTS // NX, NX), obs,
+    )(count, *map(in_hbm, (
+        vert_coef, inv_thick, owner.reshape(SLOTS // NX, NX), obs,
         cell.reshape(SLOTS // NX, NX), *coefs,
-    )
+    )))
 
 
 WAYS = 4
 
 
-def add_body(recv_ref, forcing_ref, matrix_ref, out_ref, full, acc0, acc1, acc2, acc3, cell_v, cell_s, sem):
+def add_body(full, cell_v, forcing_ref, matrix_ref, out_ref, acc0, acc1, acc2, acc3, cell_s, sem):
     accs = (acc0, acc1, acc2, acc3)
-    pick = jnp.where(
-        iota((8, NX), 1) == 16 * iota((8, NX), 0) + (LEV - 64), 1.0, 0.0
-    ).astype(F32)
-
-    def cells(b, _):
-        part = recv_ref[pl.ds(16 * b, 16), pl.ds(32, 8), :].reshape(NX, NX)
-        found = lax.dot_general(
-            pick, part, (((1,), (1,)), ((), ())), precision=HI, preferred_element_type=F32
-        )
-        cell_v[:, pl.ds(pl.multiple_of(b * NX, NX), NX)] = (found + 0.5).astype(jnp.int32)
-        return 0
-
-    lax.fori_loop(0, 8, cells, 0, unroll=True)
     copy = pltpu.make_async_copy(cell_v, cell_s, sem)
     copy.start()
-
-    def unfold(s, _):
-        rest = recv_ref[s, pl.ds(32, 8), :]
-        lane8 = iota((8, NX), 1)
-        for g in range(8):
-            tail = pltpu.roll(rest, (64 - 16 * g) % NX, 1) if g != 4 else rest
-            head = recv_ref[s, pl.ds(8 * (g % 4), 8), :]
-            head = pltpu.roll(head, 64, 1) if g >= 4 else head
-            full[pl.ds(s * CAP + 8 * g, 8), :] = jnp.where(lane8 < 64, head, tail)
-        return 0
-
-    lax.fori_loop(0, DEV, unfold, 0, unroll=4)
 
     def clear(i, _):
         at = pl.ds(pl.multiple_of(i * 64, 64), 64)
@@ -388,13 +420,11 @@
             for e in range(8):
                 for w, acc in enumerate(accs):
                     src = s + w * per
-                    cell = cell_s[g, src * 8 + e]
-                    at = pl.ds(cell, 1)
+                    at = pl.ds(cell_s[g, src * 8 + e], 1)
                     acc[at, :] = acc[at, :] + full[pl.ds(src * CAP + 8 * g + e, 1), :]
         return 0
 
     lax.fori_loop(0, per, add, 0)
-
     matrix = matrix_ref[pl.ds(0, LP), pl.ds(0, LEV)]
 
     def finish(b, _):
@@ -414,22 +444,21 @@
     lax.fori_loop(0, NY // 2, finish, 0, unroll=4)
 
 
-def add_profiles(recv, forcing, matrix):
+def add_profiles(full, cells, forcing, matrix):
     vm = pl.BlockSpec(memory_space=pltpu.VMEM)
     return pl.pallas_call(
         add_body,
         out_shape=jax.ShapeDtypeStruct((NY, LP, NX), F32),
-        in_specs=[vm, vm, vm],
+        in_specs=[vm, vm, vm, vm],
         out_specs=vm,
-        scratch_shapes=[pltpu.VMEM((SLOTS, NX), F32)] * 5
+        scratch_shapes=[pltpu.VMEM((SLOTS, NX), F32)] * 4
         + [
-            pltpu.VMEM((8, 8 * DEV), jnp.int32),
             pltpu.SMEM((8, 8 * DEV), jnp.int32),
             pltpu.SemaphoreType.DMA(()),
         ],
-        compiler_params=pltpu.CompilerParams(vmem_limit_bytes=56 << 20),
+        compiler_params=pltpu.CompilerParams(vmem_limit_bytes=30 << 20),
         name="add_profiles",
-    )(recv, forcing.reshape(LEV * NY, NX), matrix)
+    )(full, cells, forcing.reshape(LEV * NY, NX), matrix)
 
 
 def spread_body(
@@ -597,7 +626,7 @@
             pltpu.SemaphoreType.DMA((8,)),
         ],
         compiler_params=pltpu.CompilerParams(
-            collective_id=1, has_side_effects=True, vmem_limit_bytes=40 << 20
+            collective_id=1, has_side_effects=True, vmem_limit_bytes=24 << 20
         ),
         name="spread",
     )(field, fac_main, fac_strip)
@@ -608,10 +637,10 @@
     coef_east, coef_north, area_inv, sea_mask, vert_coef, inv_thick,
 ):
     coefs = (coef_east, coef_north, area_inv, sea_mask)
-    recv, fac_main, fac_strip, matrix = send_profiles(
+    full, cells, fac_main, fac_strip, matrix = send_profiles(
         obs_count, vert_coef, inv_thick, obs_owner, obs_values, obs_cell, coefs
     )
-    field = add_profiles(recv, forcing, matrix)
+    field = add_profiles(full, cells, forcing, matrix)
     return spread(field, fac_main, fac_strip).reshape(LEV, NY, NX)
 
 

time: 115 us -> 97.9 us (0.85)
  local copies, waits for them, and re-layouts: 12.9 us -> 1.44 us
  Pallas kernels: 100 us -> 95.5 us
    unnamed x25 -> x3, local copies, waits for them, and re-layouts: 12.9 us -> 1.44 us
    pallas_call x1, Pallas kernels: 30.7 us -> 22.1 us  [add_profiles(): pl.pallas_call(add_body, out_shape=jax.ShapeDtypeStruct((NY, LP, NX), F32...]
    pallas_call x1, Pallas kernels: 18.6 us -> 20.9 us  [spread(): pl.pallas_call(spread_body, out_shape=jax.ShapeDtypeStruct((LEV * NY, NX)...]
    pallas_call x1, Pallas kernels: 51.1 us -> 52.5 us  [send_profiles(): pl.pallas_call(send_body, out_shape=(jax.ShapeDtypeStruct((SLOTS, NX), F3...]
where the time goes in v3:
time: 97.9 us; the launch traced here: 97.8 us
  Pallas kernels  95.5 us (98%)
  local copies, waits for them, and re-layouts  1.44 us (1%)
    pallas_call x1, Pallas kernels, send_profiles(): pl.pallas_call(send_body, out_shape=(jax.ShapeDtypeStruct((SLOTS, NX), F3...  52.5 us
    pallas_call x1, Pallas kernels, add_profiles(): pl.pallas_call(add_body, out_shape=jax.ShapeDtypeStruct((NY, LP, NX), F32...  22.1 us
    pallas_call x1, Pallas kernels, spread(): pl.pallas_call(spread_body, out_shape=jax.ShapeDtypeStruct((LEV * NY, NX)...  20.9 us

profile of v3, /device:TPU:0, one launch (start us, length us, event | category | flops | bytes accessed | tf_op | source)
XLA Modules:
  0.0 97.8 jit_solution(18089349988639304651)
XLA Ops:
  0.0 0.0 copy-start
  0.8 52.5 %send_profiles.1 = (f32[8192,128]{1,0:T(8,128)S(1)}, s32[8,1024]{1,0:T(8,128)S(1)}, f32[5,72,128]{2,1,0:T(8,128)S(1)}, f32[5,24,128]{2,1,0:T(8,128)S(1)}, f32[128,128]{1,0:T(8,128)S(1)}) custom-call(s32[1]{0:T(128)S(6)} %copy.13.count_ref, f32[74]{0:T(128)} %vert_hbm.1, f32[75]{0:T(128)} %thick_hbm.1, s32[64,128]{1,0:T(8,128)} %bitcast.6, ...), custom_call_target="tpu_custom_call" | custom-call | tf_op jit(solution)/shard_map/send_profiles/pallas_call | solution.py:347
  53.3 0.0 copy-done
  53.3 22.1 %add_profiles.1.field_ref = f32[64,80,128]{2,1,0:T(8,128)S(1)} custom-call(f32[8192,128]{1,0:T(8,128)S(1)} %get-tuple-element.10.full, s32[8,1024]{1,0:T(8,128)S(1)} %get-tuple-element.11.cell_v, f32[4800,128]{1,0:T(8,128)S(1)} %bitcast.5, f32[128,128]{1,0:T(8,128)S(1)} %get-tuple-element.12.matrix_ref), custom_call_target="tpu_custom_call" | custom-call | tf_op jit(solution)/shard_map/add_profiles/pallas_call | solution.py:449
  75.4 20.9 %spread.1 = f32[4800,128]{1,0:T(8,128)S(1)} custom-call(f32[64,80,128]{2,1,0:T(8,128)S(1)} %add_profiles.1.field_ref, f32[5,72,128]{2,1,0:T(8,128)S(1)} %get-tuple-element.13.fac_ref, f32[5,24,128]{2,1,0:T(8,128)S(1)} %get-tuple-element.14.strip_ref), custom_call_target="tpu_custom_call" | custom-call | tf_op jit(solution)/shard_map/spread/pallas_call | solution.py:616
  96.3 1.4 %copy.14 = f32[75,64,128]{2,1,0:T(8,128)} copy(f32[75,64,128]{2,1,0:T(8,128)S(1)} %bitcast.4) | data formatting | bytes 4915200
Async XLA Ops:
  0.0 53.3 %copy-start = (f32[75,64,128]{2,1,0:T(8,128)S(1)}, f32[75,64,128]{2,1,0:T(8,128)}, u32[]{:S(2)}) copy-start(f32[75,64,128]{2,1,0:T(8,128)} %param.11) | copy-start | bytes 7372804

commit v4 on v3

--- a/solution.py
+++ b/solution.py
@@ -92,9 +92,9 @@
         return offset + prefix[:, width:], acc + found * scale
 
     zero = jnp.zeros((DEV, NX), F32)
-    _, acc = lax.fori_loop(0, SLOTS // width, step, (zero, zero), unroll=4)
+    _, acc = lax.fori_loop(0, SLOTS // width, step, (zero, zero), unroll=16)
     total = (acc + pltpu.roll(acc, CAP, 1)).astype(jnp.int32)
-    idx_ref[...] = jnp.clip(jnp.where(total > 0, total - 1, SLOTS), 0, SLOTS)
+    idx_ref[...] = jnp.clip(jnp.where(total > 0, total - 1, SLOTS + acc_lane % 8), 0, SLOTS + 7)
 
 
 def factors(coef_refs, row_halo_ref, col_halo_ref, corner_ref, coef_main, coef_side, fac_main_ref, fac_strip_ref):
@@ -230,7 +230,8 @@
         return 0
 
     lax.fori_loop(0, SLOTS // NX, turn, 0, unroll=4)
-    table[pl.ds(SLOTS, 8), :] = jnp.zeros((8, NX), F32)
+    spare = (iota((8, NX), 0) * 1024).astype(F32)
+    table[pl.ds(SLOTS, 8), :] = jnp.where(iota((8, NX), 1) == LEV, spare, 0.0)
 
     lane = iota((NY, NX), 1)
     cols = jnp.zeros((NY, NX), F32)
@@ -275,7 +276,7 @@
 
     def gather(owner):
         for k in range(CAP):
-            at = jnp.minimum(jnp.maximum(idx_ref[owner, k], 0), SLOTS)
+            at = jnp.minimum(jnp.maximum(idx_ref[owner, k], 0), SLOTS + 7)
             rows[pl.ds(k, 1), :] = table[pl.ds(at, 1), :]
 
     def fold(box):
@@ -335,7 +336,7 @@
         found = lax.dot_general(
             pick, part, (((1,), (1,)), ((), ())), precision=HI, preferred_element_type=F32
         )
-        cells_ref[:, pl.ds(NX * b, NX)] = (found + 0.5).astype(jnp.int32)
+        cells_ref[pl.ds(8 * b, 8), :] = (found + 0.5).astype(jnp.int32)
     others = pl.ds(0, DEV - 1)
     pltpu.make_async_copy(outbox.at[others], outbox.at[others], send_sem).wait()
 
@@ -348,7 +349,7 @@
         send_body,
         out_shape=(
             jax.ShapeDtypeStruct((SLOTS, NX), F32),
-            jax.ShapeDtypeStruct((8, 8 * DEV), jnp.int32),
+            jax.ShapeDtypeStruct((SLOTS // NX, NX), jnp.int32),
             jax.ShapeDtypeStruct((5, YE, NX), F32),
             jax.ShapeDtypeStruct((5, 24, NX), F32),
             jax.ShapeDtypeStruct((NX, NX), F32),
@@ -397,11 +398,11 @@
     )))
 
 
-WAYS = 4
-
-
-def add_body(full, cell_v, forcing_ref, matrix_ref, out_ref, acc0, acc1, acc2, acc3, cell_s, sem):
-    accs = (acc0, acc1, acc2, acc3)
+WAYS = 8
+
+
+def add_body(full, cell_v, forcing_ref, matrix_ref, out_ref, acc0, acc1, acc2, acc3, acc4, acc5, acc6, acc7, cell_s, sem):
+    accs = (acc0, acc1, acc2, acc3, acc4, acc5, acc6, acc7)
     copy = pltpu.make_async_copy(cell_v, cell_s, sem)
     copy.start()
 
@@ -416,12 +417,18 @@
     per = DEV // WAYS
 
     def add(s, _):
+        starts = [pl.multiple_of((s + w * per) * CAP, CAP) for w in range(WAYS)]
+        firsts = [(s + w * per) // 16 * 1024 + (s + w * per) % 16 * 8 for w in range(WAYS)]
+        blocks = [full.at[pl.ds(start, CAP), :] for start in starts]
         for g in range(8):
             for e in range(8):
-                for w, acc in enumerate(accs):
-                    src = s + w * per
-                    at = pl.ds(cell_s[g, src * 8 + e], 1)
-                    acc[at, :] = acc[at, :] + full[pl.ds(src * CAP + 8 * g + e, 1), :]
+                places_of = [pl.ds(cell_s[first + (128 * g + e)], 1) for first in firsts]
+                sums = [
+                    acc[at, :] + block[pl.ds(8 * g + e, 1), :]
+                    for acc, at, block in zip(accs, places_of, blocks)
+                ]
+                for acc, at, total in zip(accs, places_of, sums):
+                    acc[at, :] = total
         return 0
 
     lax.fori_loop(0, per, add, 0)
@@ -432,7 +439,10 @@
         for h in range(2):
             y = 2 * b + h
             at = pl.ds(pl.multiple_of(y * NX, NX), NX)
-            total = (acc0[at, :] + acc1[at, :]) + (acc2[at, :] + acc3[at, :])
+            parts = [acc[at, :] for acc in accs]
+            while len(parts) > 1:
+                parts = [p + q for p, q in zip(parts[::2], parts[1::2])]
+            total = parts[0]
             loaded.append(total.T[:LEV] + forcing_ref[pl.ds(y, LEV, stride=NY), :])
         product = jnp.dot(
             matrix, jnp.concatenate(loaded, 1), precision=HI, preferred_element_type=F32
@@ -441,7 +451,7 @@
         out_ref[2 * b + 1] = product[:, NX:]
         return 0
 
-    lax.fori_loop(0, NY // 2, finish, 0, unroll=4)
+    lax.fori_loop(0, NY // 2, finish, 0, unroll=8)
 
 
 def add_profiles(full, cells, forcing, matrix):
@@ -451,14 +461,14 @@
         out_shape=jax.ShapeDtypeStruct((NY, LP, NX), F32),
         in_specs=[vm, vm, vm, vm],
         out_specs=vm,
-        scratch_shapes=[pltpu.VMEM((SLOTS, NX), F32)] * 4
+        scratch_shapes=[pltpu.VMEM((SLOTS, NX), F32)] * 8
         + [
-            pltpu.SMEM((8, 8 * DEV), jnp.int32),
+            pltpu.SMEM((SLOTS,), jnp.int32),
             pltpu.SemaphoreType.DMA(()),
         ],
-        compiler_params=pltpu.CompilerParams(vmem_limit_bytes=30 << 20),
+        compiler_params=pltpu.CompilerParams(vmem_limit_bytes=44 << 20),
         name="add_profiles",
-    )(full, cells, forcing.reshape(LEV * NY, NX), matrix)
+    )(full, cells.reshape(SLOTS), forcing.reshape(LEV * NY, NX), matrix)
 
 
 def spread_body(

time: 97.9 us -> 89.3 us (0.912)
  Pallas kernels: 95.5 us -> 86.9 us
    pallas_call x1, Pallas kernels: 22.1 us -> 14.5 us  [add_profiles(): pl.pallas_call(add_body, out_shape=jax.ShapeDtypeStruct((NY, LP, NX), F32...]
where the time goes in v4:
time: 89.3 us; the launch traced here: 89.2 us
  Pallas kernels  86.9 us (97%)
  local copies, waits for them, and re-layouts  1.44 us (2%)
    pallas_call x1, Pallas kernels, send_profiles(): pl.pallas_call(send_body, out_shape=(jax.ShapeDtypeStruct((SLOTS, NX), F3...  51.6 us
    pallas_call x1, Pallas kernels, spread(): pl.pallas_call(spread_body, out_shape=jax.ShapeDtypeStruct((LEV * NY, NX)...  20.8 us
    pallas_call x1, Pallas kernels, add_profiles(): pl.pallas_call(add_body, out_shape=jax.ShapeDtypeStruct((NY, LP, NX), F32...  14.5 us

profile of v4, /device:TPU:0, one launch (start us, length us, event | category | flops | bytes accessed | tf_op | source)
XLA Modules:
  0.0 89.2 jit_solution(4225680114530458832)
XLA Ops:
  0.0 0.0 copy-start
  0.8 51.6 %send_profiles.1 = (f32[8192,128]{1,0:T(8,128)S(1)}, s32[64,128]{1,0:T(8,128)S(1)}, f32[5,72,128]{2,1,0:T(8,128)S(1)}, f32[5,24,128]{2,1,0:T(8,128)S(1)}, f32[128,128]{1,0:T(8,128)S(1)}) custom-call(s32[1]{0:T(128)S(6)} %copy.13.count_ref, f32[74]{0:T(128)} %vert_hbm.1, f32[75]{0:T(128)} %thick_hbm.1, s32[64,128]{1,0:T(8,128)} %bitcast.8, ...), custom_call_target="tpu_custom_call" | custom-call | tf_op jit(solution)/shard_map/send_profiles/pallas_call | solution.py:348
  52.4 0.0 copy-done
  52.4 14.5 %add_profiles.1.field_ref = f32[64,80,128]{2,1,0:T(8,128)S(1)} custom-call(f32[8192,128]{1,0:T(8,128)S(1)} %get-tuple-element.10.full, s32[8192]{0:T(1024)S(1)} %bitcast.7, f32[4800,128]{1,0:T(8,128)S(1)} %bitcast.6, f32[128,128]{1,0:T(8,128)S(1)} %get-tuple-element.12.matrix_ref), custom_call_target="tpu_custom_call" | custom-call | tf_op jit(solution)/shard_map/add_profiles/pallas_call | solution.py:459
  66.9 20.8 %spread.1 = f32[4800,128]{1,0:T(8,128)S(1)} custom-call(f32[64,80,128]{2,1,0:T(8,128)S(1)} %add_profiles.1.field_ref, f32[5,72,128]{2,1,0:T(8,128)S(1)} %get-tuple-element.13.fac_ref, f32[5,24,128]{2,1,0:T(8,128)S(1)} %get-tuple-element.14.strip_ref), custom_call_target="tpu_custom_call" | custom-call | tf_op jit(solution)/shard_map/spread/pallas_call | solution.py:626
  87.7 1.4 %copy.14 = f32[75,64,128]{2,1,0:T(8,128)} copy(f32[75,64,128]{2,1,0:T(8,128)S(1)} %bitcast.5) | data formatting | bytes 4915200
Async XLA Ops:
  0.0 52.4 %copy-start = (f32[75,64,128]{2,1,0:T(8,128)S(1)}, f32[75,64,128]{2,1,0:T(8,128)}, u32[]{:S(2)}) copy-start(f32[75,64,128]{2,1,0:T(8,128)} %param.11) | copy-start | bytes 7372804

commit v5 on v4

--- a/solution.py
+++ b/solution.py
@@ -172,9 +172,19 @@
         fac_strip_ref[i, pl.ds(0, Q), :] = jnp.where(gap, 0.0, strip)
 
 
+def clear(refs):
+    def some(i, _):
+        at = pl.ds(pl.multiple_of(i * 64, 64), 64)
+        for ref in refs:
+            ref[at, :] = jnp.zeros((64, NX), F32)
+        return 0
+
+    lax.fori_loop(0, SLOTS // 64, some, 0, unroll=2)
+
+
 def send_body(
     count_ref, vert_hbm, thick_hbm, own_hbm, obs_hbm, cell_hbm, east_hbm, north_hbm, area_hbm, sea_hbm,
-    full_ref, cells_ref, fac_main_ref, fac_strip_ref, matrix_ref,
+    full_ref, cells_ref, fac_main_ref, fac_strip_ref, matrix_ref, sum0, sum1, sum2, sum3,
     vert_ref, thick_ref, own_ref, obs_ref, cell_ref, east_ref, north_ref, area_ref, sea_ref,
     recv, load_sem, table, rows, outbox, coef_box, colbox, row_halo, col_halo, corner, coef_main, coef_side,
     cp_ref, dp_ref, idx_v, idx_ref, idx_sem, send_sem, recv_sem, side_send, side_recv,
@@ -309,6 +319,8 @@
     for copy in side:
         copy.wait()
     factors(coef_refs, row_halo, col_halo, corner, coef_main, coef_side, fac_main_ref, fac_strip_ref)
+    clear((sum0, sum1, sum2, sum3))
+
     pick = jnp.where(
         iota((8, NX), 1) == 16 * iota((8, NX), 0) + (LEV - 64), 1.0, 0.0
     ).astype(F32)
@@ -353,9 +365,9 @@
             jax.ShapeDtypeStruct((5, YE, NX), F32),
             jax.ShapeDtypeStruct((5, 24, NX), F32),
             jax.ShapeDtypeStruct((NX, NX), F32),
-        ),
+        ) + (jax.ShapeDtypeStruct((SLOTS, NX), F32),) * EARLY,
         in_specs=[sm] + [pl.BlockSpec(memory_space=pltpu.HBM)] * 9,
-        out_specs=(vm,) * 5,
+        out_specs=(vm,) * (5 + EARLY),
         scratch_shapes=[
             pltpu.SMEM((LEV - 1,), F32),
             pltpu.SMEM((LEV,), F32),
@@ -389,7 +401,7 @@
             pltpu.SemaphoreType.DMA((8,)),
         ],
         compiler_params=pltpu.CompilerParams(
-            collective_id=0, has_side_effects=True, vmem_limit_bytes=24 << 20
+            collective_id=0, has_side_effects=True, vmem_limit_bytes=18 << 20
         ),
         name="send_profiles",
     )(count, *map(in_hbm, (
@@ -399,20 +411,18 @@
 
 
 WAYS = 8
-
-
-def add_body(full, cell_v, forcing_ref, matrix_ref, out_ref, acc0, acc1, acc2, acc3, acc4, acc5, acc6, acc7, cell_s, sem):
+EARLY = 4
+
+
+def add_body(
+    full, cell_v, forcing_ref, matrix_ref, in0, in1, in2, in3, out_ref,
+    acc0, acc1, acc2, acc3, acc4, acc5, acc6, acc7, cell_s, sem,
+):
     accs = (acc0, acc1, acc2, acc3, acc4, acc5, acc6, acc7)
     copy = pltpu.make_async_copy(cell_v, cell_s, sem)
     copy.start()
 
-    def clear(i, _):
-        at = pl.ds(pl.multiple_of(i * 64, 64), 64)
-        for acc in accs:
-            acc[at, :] = jnp.zeros((64, NX), F32)
-        return 0
-
-    lax.fori_loop(0, SLOTS // 64, clear, 0, unroll=2)
+    clear(accs[EARLY:])
     copy.wait()
     per = DEV // WAYS
 
@@ -432,7 +442,11 @@
         return 0
 
     lax.fori_loop(0, per, add, 0)
-    matrix = matrix_ref[pl.ds(0, LP), pl.ds(0, LEV)]
+    whole = matrix_ref[pl.ds(0, LP), pl.ds(0, LP)]
+    high = whole.astype(BF16)
+    low = (whole - high.astype(F32)).astype(BF16)
+    matrix = jnp.concatenate([high, high, low], 1)
+    padding = jnp.zeros((LP - LEV, NX), F32)
 
     def finish(b, _):
         loaded = []
@@ -443,10 +457,13 @@
             while len(parts) > 1:
                 parts = [p + q for p, q in zip(parts[::2], parts[1::2])]
             total = parts[0]
-            loaded.append(total.T[:LEV] + forcing_ref[pl.ds(y, LEV, stride=NY), :])
-        product = jnp.dot(
-            matrix, jnp.concatenate(loaded, 1), precision=HI, preferred_element_type=F32
-        )
+            column = total.T[:LEV] + forcing_ref[pl.ds(y, LEV, stride=NY), :]
+            loaded.append(jnp.concatenate([column, padding], 0))
+        values = jnp.concatenate(loaded, 1)
+        top = values.astype(BF16)
+        rest = (values - top.astype(F32)).astype(BF16)
+        parts = jnp.concatenate([top, rest, top], 0)
+        product = jnp.dot(matrix, parts, preferred_element_type=F32)
         out_ref[2 * b] = product[:, :NX]
         out_ref[2 * b + 1] = product[:, NX:]
         return 0
@@ -454,27 +471,29 @@
     lax.fori_loop(0, NY // 2, finish, 0, unroll=8)
 
 
-def add_profiles(full, cells, forcing, matrix):
+def add_profiles(full, cells, forcing, matrix, sums):
     vm = pl.BlockSpec(memory_space=pltpu.VMEM)
     return pl.pallas_call(
         add_body,
-        out_shape=jax.ShapeDtypeStruct((NY, LP, NX), F32),
-        in_specs=[vm, vm, vm, vm],
-        out_specs=vm,
-        scratch_shapes=[pltpu.VMEM((SLOTS, NX), F32)] * 8
+        out_shape=(jax.ShapeDtypeStruct((NY, LP, NX), F32),)
+        + (jax.ShapeDtypeStruct((SLOTS, NX), F32),) * EARLY,
+        in_specs=[vm] * (4 + EARLY),
+        out_specs=(vm,) * (1 + EARLY),
+        input_output_aliases={4 + w: 1 + w for w in range(EARLY)},
+        scratch_shapes=[pltpu.VMEM((SLOTS, NX), F32)] * (WAYS - EARLY)
         + [
             pltpu.SMEM((SLOTS,), jnp.int32),
             pltpu.SemaphoreType.DMA(()),
         ],
-        compiler_params=pltpu.CompilerParams(vmem_limit_bytes=44 << 20),
+        compiler_params=pltpu.CompilerParams(vmem_limit_bytes=22 << 20),
         name="add_profiles",
-    )(full, cells.reshape(SLOTS), forcing.reshape(LEV * NY, NX), matrix)
+    )(full, cells.reshape(SLOTS), forcing.reshape(LEV * NY, NX), matrix, *sums)[0]
 
 
 def spread_body(
     field_ref, fac_ref, strip_ref,
     out_ref,
-    wide_a, wide_b, tips, strip_a, strip_b, east_box, west_box, from_west, from_east, corners,
+    wide_a, wide_b, tips, strip_a, strip_b, east_box, west_box, from_west, from_east, corner_box, corners,
     own_sem, send_sem, recv_sem,
 ):
     lon = lax.axis_index("lon")
@@ -520,16 +539,26 @@
         east_box[b] = e
         west_box[b] = w
 
+    lane16 = iota((16, NX), 1)
+    for number, (box, start) in enumerate(
+        ((east_box.at[1], 104), (west_box.at[1], 104), (east_box.at[0], 16), (west_box.at[0], 16))
+    ):
+        total = jnp.zeros((16, NX), F32)
+        for h in range(LP // 16):
+            piece = pltpu.roll(box[pl.ds(16 * h, 16), :], (16 * h - start) % NX, 1)
+            total = jnp.where(lane16 // 16 == h, piece, total)
+        corner_box[number] = total
+
     pl.semaphore_wait(barrier, 8)
     moves = [
         (field_ref.at[pl.ds(NY - HALO, HALO)], wide_a.at[pl.ds(0, HALO)]),
         (field_ref.at[pl.ds(0, HALO)], wide_a.at[pl.ds(NY + HALO, HALO)]),
         (east_box, from_west),
         (west_box, from_east),
-        (east_box.at[1], corners.at[0]),
-        (west_box.at[1], corners.at[1]),
-        (east_box.at[0], corners.at[2]),
-        (west_box.at[0], corners.at[3]),
+        (corner_box.at[0], corners.at[0]),
+        (corner_box.at[1], corners.at[1]),
+        (corner_box.at[2], corners.at[2]),
+        (corner_box.at[3], corners.at[3]),
     ]
     copies = []
     for number, (src, dst) in enumerate(moves):
@@ -571,9 +600,17 @@
 
     for near, from_side in ((0, from_west), (1, from_east)):
         below, above = corners[near], corners[near + 2]
-        from_side[0] = jnp.where(lane < 16, pltpu.roll(below, 24, 1), from_side[0])
-        from_side[1] = jnp.where(lane >= 120, pltpu.roll(above, 104, 1), from_side[1])
-        from_side[2] = jnp.where((lane >= 96) & (lane < 104), pltpu.roll(above, 72, 1), from_side[2])
+        for h in range(LP // 16):
+            at = pl.ds(16 * h, 16)
+
+            def put(box, keep, corner, shift, at=at, from_side=from_side):
+                box_rows = from_side[box, at, :]
+                piece = pltpu.roll(corner, shift % NX, 1) if shift % NX else corner
+                from_side[box, at, :] = jnp.where(keep, piece, box_rows)
+
+            put(0, lane16 < 16, below, -16 * h)
+            put(1, lane16 >= 120, above, 120 - 16 * h)
+            put(2, (lane16 >= 96) & (lane16 < 104), above, 88 - 16 * h)
     for h in range(HALO):
         q = Q - HALO + h
         tips[h] = jnp.where((group == 0) & (place < 16), pltpu.roll(wide_a[h], 8, 1), tips[h])
@@ -630,7 +667,8 @@
         out_specs=vm,
         scratch_shapes=[
             wide, wide, pltpu.VMEM((Q, LP, NX), F32), strip, strip, box, box, box, box,
-            pltpu.VMEM((4, LP, NX), F32),
+            pltpu.VMEM((4, 16, NX), F32),
+            pltpu.VMEM((4, 16, NX), F32),
             pltpu.SemaphoreType.DMA(()),
             pltpu.SemaphoreType.DMA((8,)),
             pltpu.SemaphoreType.DMA((8,)),
@@ -647,10 +685,10 @@
     coef_east, coef_north, area_inv, sea_mask, vert_coef, inv_thick,
 ):
     coefs = (coef_east, coef_north, area_inv, sea_mask)
-    full, cells, fac_main, fac_strip, matrix = send_profiles(
+    full, cells, fac_main, fac_strip, matrix, *sums = send_profiles(
         obs_count, vert_coef, inv_thick, obs_owner, obs_values, obs_cell, coefs
     )
-    field = add_profiles(full, cells, forcing, matrix)
+    field = add_profiles(full, cells, forcing, matrix, sums)
     return spread(field, fac_main, fac_strip).reshape(LEV, NY, NX)
 
 

time: 89.3 us -> 87.1 us (0.975)
  Pallas kernels: 86.9 us -> 84.7 us
    pallas_call x1, Pallas kernels: 14.5 us -> 12.8 us  [add_profiles(): pl.pallas_call(add_body, out_shape=(jax.ShapeDtypeStruct((NY, LP, NX), F3...]
where the time goes in v5:
time: 87.1 us; the launch traced here: 87 us
  Pallas kernels  84.7 us (97%)
  local copies, waits for them, and re-layouts  1.44 us (2%)
    pallas_call x1, Pallas kernels, send_profiles(): pl.pallas_call(send_body, out_shape=(jax.ShapeDtypeStruct((SLOTS, NX), F3...  51.6 us
    pallas_call x1, Pallas kernels, spread(): pl.pallas_call(spread_body, out_shape=jax.ShapeDtypeStruct((LEV * NY, NX)...  20.4 us
    pallas_call x1, Pallas kernels, add_profiles(): pl.pallas_call(add_body, out_shape=(jax.ShapeDtypeStruct((NY, LP, NX), F3...  12.8 us

profile of v5, /device:TPU:0, one launch (start us, length us, event | category | flops | bytes accessed | tf_op | source)
XLA Modules:
  0.0 87.0 jit_solution(14933518332197316187)
XLA Ops:
  0.0 0.0 copy-start
  0.8 51.6 %send_profiles.1 = (f32[8192,128]{1,0:T(8,128)S(1)}, s32[64,128]{1,0:T(8,128)S(1)}, f32[5,72,128]{2,1,0:T(8,128)S(1)}, f32[5,24,128]{2,1,0:T(8,128)S(1)}, f32[12...) custom-call(s32[1]{0:T(128)S(6)} %copy.21.count_ref, ...), custom_call_target="tpu_custom_call" | custom-call | tf_op jit(solution)/shard_map/send_profiles/pallas_call | solution.py:360
  52.4 0.0 copy-done
  52.4 12.8 %add_profiles.1 = (f32[64,80,128]{2,1,0:T(8,128)S(1)}, f32[8192,128]{1,0:T(8,128)S(1)}, f32[8192,128]{1,0:T(8,128)S(1)}, f32[8192,128]{1,0:T(8,128)S(1)}, f32[8192,128]{1,0:T(8,128)S(1)}) custom-call(f32[8192,128]{1,0:T(8,128)S(1)} %get-tuple-element.15.full, ...), custom_call_target="tpu_custom_call", output_to_operand_aliasing={{1}: (4, {}), {2}: (5, {}), {3}: (6, {}), {4}: (7, {})} | custom-call | tf_op jit(solution)/shard_map/add_profiles/pallas_call | solution.py:476
  65.2 20.4 %spread.1 = f32[4800,128]{1,0:T(8,128)S(1)} custom-call(f32[64,80,128]{2,1,0:T(8,128)S(1)} %get-tuple-element.22.field_ref, f32[5,72,128]{2,1,0:T(8,128)S(1)} %get-tuple-element.23.fac_ref, f32[5,24,128]{2,1,0:T(8,128)S(1)} %get-tuple-element.24.strip_ref), custom_call_target="tpu_custom_call" | custom-call | tf_op jit(solution)/shard_map/spread/pallas_call | solution.py:663
  85.5 1.4 %copy.22 = f32[75,64,128]{2,1,0:T(8,128)} copy(f32[75,64,128]{2,1,0:T(8,128)S(1)} %bitcast.5) | data formatting | bytes 4915200
Async XLA Ops:
  0.0 52.4 %copy-start = (f32[75,64,128]{2,1,0:T(8,128)S(1)}, f32[75,64,128]{2,1,0:T(8,128)}, u32[]{:S(2)}) copy-start(f32[75,64,128]{2,1,0:T(8,128)} %param.11) | copy-start | bytes 7372804

commit v6 on v5

--- a/solution.py
+++ b/solution.py
@@ -213,11 +213,19 @@
 
     barrier = pltpu.get_barrier_semaphore()
 
-    def greet(k, _):
-        pl.semaphore_signal(barrier, inc=1, device_id=target(k), device_id_type=MESH)
-        return 0
-
-    lax.fori_loop(1, DEV, greet, 0)
+    deep = [lax.rem(z + d, 4) * 8 for d in range(4)]
+    wide = [lax.rem(y + d, 4) * 2 for d in range(4)]
+    core = [lax.rem(c + d, 2) for d in range(2)]
+    flat = [lax.rem(lat + d, 4) for d in range(4)]
+    for a in range(4):
+        for b in range(4):
+            for d in range(2):
+                there = deep[a] + wide[b] + core[d]
+                for e in range(4):
+                    if a + b + d + e:
+                        pl.semaphore_signal(
+                            barrier, inc=1, device_id=(there, flat[e]), device_id_type=MESH
+                        )
 
     loads[0].wait()
     places(count_ref[0], own_ref, idx_v)

time: 87.1 us -> 84.1 us (0.966)
  Pallas kernels: 84.7 us -> 81.7 us
    pallas_call x1, Pallas kernels: 51.6 us -> 48.5 us  [send_profiles(): pl.pallas_call(send_body, out_shape=(jax.ShapeDtypeStruct((SLOTS, NX), F3...]
where the time goes in v6:
time: 84.1 us; the launch traced here: 84 us
  Pallas kernels  81.7 us (97%)
  local copies, waits for them, and re-layouts  1.44 us (2%)
    pallas_call x1, Pallas kernels, send_profiles(): pl.pallas_call(send_body, out_shape=(jax.ShapeDtypeStruct((SLOTS, NX), F3...  48.5 us
    pallas_call x1, Pallas kernels, spread(): pl.pallas_call(spread_body, out_shape=jax.ShapeDtypeStruct((LEV * NY, NX)...  20.4 us
    pallas_call x1, Pallas kernels, add_profiles(): pl.pallas_call(add_body, out_shape=(jax.ShapeDtypeStruct((NY, LP, NX), F3...  12.8 us

profile of v6, /device:TPU:0, one launch (start us, length us, event | category | flops | bytes accessed | tf_op | source)
XLA Modules:
  0.0 84.0 jit_solution(9119617828814011860)
XLA Ops:
  0.0 0.0 copy-start
  0.8 48.5 %send_profiles.1 = (f32[8192,128]{1,0:T(8,128)S(1)}, s32[64,128]{1,0:T(8,128)S(1)}, f32[5,72,128]{2,1,0:T(8,128)S(1)}, f32[5,24,128]{2,1,0:T(8,128)S(1)}, f32[12...) custom-call(s32[1]{0:T(128)S(6)} %copy.21.count_ref, ...), custom_call_target="tpu_custom_call" | custom-call | tf_op jit(solution)/shard_map/send_profiles/pallas_call | solution.py:368
  49.3 0.0 copy-done
  49.3 12.8 %add_profiles.1 = (f32[64,80,128]{2,1,0:T(8,128)S(1)}, f32[8192,128]{1,0:T(8,128)S(1)}, f32[8192,128]{1,0:T(8,128)S(1)}, f32[8192,128]{1,0:T(8,128)S(1)}, f32[8192,128]{1,0:T(8,128)S(1)}) custom-call(f32[8192,128]{1,0:T(8,128)S(1)} %get-tuple-element.15.full, ...), custom_call_target="tpu_custom_call", output_to_operand_aliasing={{1}: (4, {}), {2}: (5, {}), {3}: (6, {}), {4}: (7, {})} | custom-call | tf_op jit(solution)/shard_map/add_profiles/pallas_call | solution.py:484
  62.1 20.4 %spread.1 = f32[4800,128]{1,0:T(8,128)S(1)} custom-call(f32[64,80,128]{2,1,0:T(8,128)S(1)} %get-tuple-element.22.field_ref, f32[5,72,128]{2,1,0:T(8,128)S(1)} %get-tuple-element.23.fac_ref, f32[5,24,128]{2,1,0:T(8,128)S(1)} %get-tuple-element.24.strip_ref), custom_call_target="tpu_custom_call" | custom-call | tf_op jit(solution)/shard_map/spread/pallas_call | solution.py:671
  82.6 1.4 %copy.22 = f32[75,64,128]{2,1,0:T(8,128)} copy(f32[75,64,128]{2,1,0:T(8,128)S(1)} %bitcast.5) | data formatting | bytes 4915200
Async XLA Ops:
  0.0 49.3 %copy-start = (f32[75,64,128]{2,1,0:T(8,128)S(1)}, f32[75,64,128]{2,1,0:T(8,128)}, u32[]{:S(2)}) copy-start(f32[75,64,128]{2,1,0:T(8,128)} %param.11) | copy-start | bytes 7372804

commit v7 on v6

--- a/solution.py
+++ b/solution.py
@@ -16,7 +16,7 @@
 HALO = 4
 YE = NY + 2 * HALO
 Q = 18
-STRIDE = 27
+STRIDE = 59
 F32 = jnp.float32
 BF16 = jnp.bfloat16
 HI = lax.Precision.HIGHEST

time: 84.1 us -> 83.8 us (level)
  no operation moved by 1% of the time
where the time goes in v7:
time: 83.8 us; the launch traced here: 83.7 us
  Pallas kernels  81.4 us (97%)
  local copies, waits for them, and re-layouts  1.44 us (2%)
    pallas_call x1, Pallas kernels, send_profiles(): pl.pallas_call(send_body, out_shape=(jax.ShapeDtypeStruct((SLOTS, NX), F3...  48.5 us
    pallas_call x1, Pallas kernels, spread(): pl.pallas_call(spread_body, out_shape=jax.ShapeDtypeStruct((LEV * NY, NX)...  19.9 us
    pallas_call x1, Pallas kernels, add_profiles(): pl.pallas_call(add_body, out_shape=(jax.ShapeDtypeStruct((NY, LP, NX), F3...  12.9 us

profile of v7, /device:TPU:0, one launch (start us, length us, event | category | flops | bytes accessed | tf_op | source)
XLA Modules:
  0.0 83.7 jit_solution(296064502859367959)
XLA Ops:
  0.0 0.0 copy-start
  0.8 48.5 %send_profiles.1 = (f32[8192,128]{1,0:T(8,128)S(1)}, s32[64,128]{1,0:T(8,128)S(1)}, f32[5,72,128]{2,1,0:T(8,128)S(1)}, f32[5,24,128]{2,1,0:T(8,128)S(1)}, f32[12...) custom-call(s32[1]{0:T(128)S(6)} %copy.21.count_ref, ...), custom_call_target="tpu_custom_call" | custom-call | tf_op jit(solution)/shard_map/send_profiles/pallas_call | solution.py:368
  49.4 0.0 copy-done
  49.4 12.9 %add_profiles.1 = (f32[64,80,128]{2,1,0:T(8,128)S(1)}, f32[8192,128]{1,0:T(8,128)S(1)}, f32[8192,128]{1,0:T(8,128)S(1)}, f32[8192,128]{1,0:T(8,128)S(1)}, f32[8192,128]{1,0:T(8,128)S(1)}) custom-call(f32[8192,128]{1,0:T(8,128)S(1)} %get-tuple-element.15.full, ...), custom_call_target="tpu_custom_call", output_to_operand_aliasing={{1}: (4, {}), {2}: (5, {}), {3}: (6, {}), {4}: (7, {})} | custom-call | tf_op jit(solution)/shard_map/add_profiles/pallas_call | solution.py:484
  62.3 19.9 %spread.1 = f32[4800,128]{1,0:T(8,128)S(1)} custom-call(f32[64,80,128]{2,1,0:T(8,128)S(1)} %get-tuple-element.22.field_ref, f32[5,72,128]{2,1,0:T(8,128)S(1)} %get-tuple-element.23.fac_ref, f32[5,24,128]{2,1,0:T(8,128)S(1)} %get-tuple-element.24.strip_ref), custom_call_target="tpu_custom_call" | custom-call | tf_op jit(solution)/shard_map/spread/pallas_call | solution.py:671
  82.2 1.4 %copy.22 = f32[75,64,128]{2,1,0:T(8,128)} copy(f32[75,64,128]{2,1,0:T(8,128)S(1)} %bitcast.5) | data formatting | bytes 4915200
Async XLA Ops:
  0.0 49.4 %copy-start = (f32[75,64,128]{2,1,0:T(8,128)S(1)}, f32[75,64,128]{2,1,0:T(8,128)}, u32[]{:S(2)}) copy-start(f32[75,64,128]{2,1,0:T(8,128)} %param.11) | copy-start | bytes 7372804

commit v8 on v7

--- a/solution.py
+++ b/solution.py
@@ -642,7 +642,7 @@
             dst[q + 1] = stencil(strip_ref, q, src, q + 1)
             return 0
 
-        lax.fori_loop(0, Q, strip, 0, unroll=6)
+        lax.fori_loop(0, Q, strip, 0, unroll=9)
 
     edge = (lane < HALO) | (lane >= NX - HALO)
 
@@ -656,7 +656,7 @@
                 out_ref[pl.ds(y - HALO, LEV, stride=NY), :] = whole[:LEV]
             return 0
 
-        lax.fori_loop(low, high, one, 0, unroll=2)
+        lax.fori_loop(low, high, one, 0, unroll=4)
 
     write(0, HALO, (1, 2, 3))
     write(HALO, Q - HALO, (0, 1, 2, 3))

time: 83.8 us -> 83.3 us (level)
  no operation moved by 1% of the time
where the time goes in v8:
time: 83.3 us
  Pallas kernels  81.1 us (97%)
  local copies, waits for them, and re-layouts  1.44 us (2%)
    pallas_call x1, Pallas kernels, send_profiles(): pl.pallas_call(send_body, out_shape=(jax.ShapeDtypeStruct((SLOTS, NX), F3...  48.5 us
    pallas_call x1, Pallas kernels, spread(): pl.pallas_call(spread_body, out_shape=jax.ShapeDtypeStruct((LEV * NY, NX)...  19.5 us
    pallas_call x1, Pallas kernels, add_profiles(): pl.pallas_call(add_body, out_shape=(jax.ShapeDtypeStruct((NY, LP, NX), F3...  13 us

profile of v8, /device:TPU:0, one launch (start us, length us, event | category | flops | bytes accessed | tf_op | source)
XLA Modules:
  0.0 83.3 jit_solution(7432946584263496014)
XLA Ops:
  0.0 0.0 copy-start
  0.8 48.5 %send_profiles.1 = (f32[8192,128]{1,0:T(8,128)S(1)}, s32[64,128]{1,0:T(8,128)S(1)}, f32[5,72,128]{2,1,0:T(8,128)S(1)}, f32[5,24,128]{2,1,0:T(8,128)S(1)}, f32[12...) custom-call(s32[1]{0:T(128)S(6)} %copy.21.count_ref, ...), custom_call_target="tpu_custom_call" | custom-call | tf_op jit(solution)/shard_map/send_profiles/pallas_call | solution.py:368
  49.4 0.0 copy-done
  49.4 13.0 %add_profiles.1 = (f32[64,80,128]{2,1,0:T(8,128)S(1)}, f32[8192,128]{1,0:T(8,128)S(1)}, f32[8192,128]{1,0:T(8,128)S(1)}, f32[8192,128]{1,0:T(8,128)S(1)}, f32[8192,128]{1,0:T(8,128)S(1)}) custom-call(f32[8192,128]{1,0:T(8,128)S(1)} %get-tuple-element.15.full, ...), custom_call_target="tpu_custom_call", output_to_operand_aliasing={{1}: (4, {}), {2}: (5, {}), {3}: (6, {}), {4}: (7, {})} | custom-call | tf_op jit(solution)/shard_map/add_profiles/pallas_call | solution.py:484
  62.4 19.5 %spread.1 = f32[4800,128]{1,0:T(8,128)S(1)} custom-call(f32[64,80,128]{2,1,0:T(8,128)S(1)} %get-tuple-element.22.field_ref, f32[5,72,128]{2,1,0:T(8,128)S(1)} %get-tuple-element.23.fac_ref, f32[5,24,128]{2,1,0:T(8,128)S(1)} %get-tuple-element.24.strip_ref), custom_call_target="tpu_custom_call" | custom-call | tf_op jit(solution)/shard_map/spread/pallas_call | solution.py:671
  81.9 1.4 %copy.22 = f32[75,64,128]{2,1,0:T(8,128)} copy(f32[75,64,128]{2,1,0:T(8,128)S(1)} %bitcast.5) | data formatting | bytes 4915200
Async XLA Ops:
  0.0 49.4 %copy-start = (f32[75,64,128]{2,1,0:T(8,128)S(1)}, f32[75,64,128]{2,1,0:T(8,128)}, u32[]{:S(2)}) copy-start(f32[75,64,128]{2,1,0:T(8,128)} %param.11) | copy-start | bytes 7372804
